TPU v7x, 512 devices: a whole 4x8x8 slice. The times are simulated.
512 devices in a mesh: dp: 4 (over z_lo, core), seq: 8 (over y), vocab: 16 (over z_hi, x).
Axes of the slice: x: 4, y: 8, z: 8 (z_hi: 4, z_lo: 2; z = z_hi * 2 + z_lo), core: 2. Of those that a mesh axis runs over, the one named last changes fastest.
Arguments:
- queries: bfloat16 [4, 256, 4096], P('dp', 'seq', 'vocab'), may hold values from -64 to 64
- enc_keys: bfloat16 [4, 1024, 4096], P('dp', 'seq', 'vocab'), may hold values from -6 to 6
- enc_values: bfloat16 [4, 1024, 4096], P('dp', 'seq', 'vocab'), may hold values from -6 to 6
- enc_lengths: int32 [4], P('dp'), may hold values from 256 to 1024, as said below
- out_proj: bfloat16 [4096, 4096], P('vocab', 'seq'), may hold values from -0.375 to 0.375
- residual: bfloat16 [4, 256, 4096], P('dp', None, 'seq'), may hold values from -270 to 270
- norm_gain: float32 [4096], P('seq'), may hold values from 0.4 to 1.6
- head_weight: bfloat16 [4096, 32128], P('seq', 'vocab'), may hold values from -1 to 1
- targets: int32 [4, 256], P('dp', 'seq'), may hold values from 0 to 32127
Outputs:
- mean_loss: float32 [], replicated
- head_grad: bfloat16 [4096, 32128], P('seq', 'vocab')
- key_grad: float32 [4, 1024, 4096], P('dp', 'seq', 'vocab')
- value_grad: float32 [4, 1024, 4096], P('dp', 'seq', 'vocab')
Inputs may be any that keep to these rules, and one draw needn't show every extreme that they name: `enc_lengths`: each example has at least 256 unpadded positions; some example has none padded.
All inputs are finite; a program needn't handle non-finite values.
Results may differ from a plain program's by a relative error of at most 0.02.
Values may be sent and summed in bfloat16 or wider, within the bound.
A program may use at most 64 MiB of HBM per device.

v0:
```python
import jax
import jax.numpy as jnp
from jax import lax
from jax.sharding import PartitionSpec as P

D = 4096
HDIM = 256


zloss_weight = 0.0001
norm_epsilon = 1e-06


def body(
    queries, enc_keys, enc_values, enc_lengths, out_proj, residual, norm_gain, head_weight, targets
):
    examples, tgt_rows, features = queries.shape
    heads_here = features // HDIM
    vocab_cols = head_weight.shape[1]
    all_targets = tgt_rows * lax.axis_size("seq")
    score_scale = HDIM ** (-0.5)
    key_all, value_all = (
        lax.all_gather(enc_keys, "seq", axis=1, tiled=True),
        lax.all_gather(enc_values, "seq", axis=1, tiled=True),
    )
    enc_rows = key_all.shape[1]
    query_heads = queries.reshape(examples, tgt_rows, heads_here, HDIM)
    key_heads = key_all.reshape(examples, enc_rows, heads_here, HDIM)
    value_heads = value_all.reshape(examples, enc_rows, heads_here, HDIM)
    scores = (
        jnp.einsum("bthd,bjhd->bhtj", query_heads, key_heads, preferred_element_type=jnp.float32)
        * score_scale
    )
    valid_keys = lax.broadcasted_iota(jnp.int32, (examples, enc_rows), 1) < enc_lengths[:, None]
    scores = jnp.where(valid_keys[:, None, None, :], scores, -jnp.inf)
    score_peak = jnp.max(scores, axis=-1, keepdims=True)
    score_exp = jnp.exp(scores - score_peak)
    weights_full = score_exp / jnp.sum(score_exp, axis=-1, keepdims=True)
    weights_half = weights_full.astype(jnp.bfloat16)
    attended = jnp.einsum(
        "bhtj,bjhd->tbhd", weights_half, value_heads, preferred_element_type=jnp.float32
    )
    attended = attended.astype(jnp.bfloat16).reshape(tgt_rows, examples, features)
    attended_all = lax.all_gather(attended, "seq", axis=0, tiled=True)
    mixed_part = jnp.einsum(
        "tbf,fd->tbd", attended_all, out_proj, preferred_element_type=jnp.float32
    )
    mixed_rows = lax.psum(mixed_part, "vocab") + jnp.swapaxes(residual, 0, 1).astype(jnp.float32)
    square_sum = lax.psum(jnp.sum(mixed_rows * mixed_rows, axis=-1), "seq")
    inverse_rms = lax.rsqrt(square_sum / D + norm_epsilon)
    normed = (mixed_rows * inverse_rms[..., None] * norm_gain).astype(jnp.bfloat16)
    row_block = normed
    logits = lax.psum_scatter(
        jnp.einsum("tbd,dv->tbv", row_block, head_weight, preferred_element_type=jnp.float32),
        "seq",
        scatter_dimension=0,
        tiled=True,
    )
    column_ids = (
        lax.broadcasted_iota(jnp.int32, (1, 1, vocab_cols), 2)
        + lax.axis_index("vocab") * vocab_cols
    )
    target_hit = column_ids == jnp.swapaxes(targets, 0, 1)[..., None]
    local_target = jnp.sum(jnp.where(target_hit, logits, 0.0), axis=-1)
    row_peak = lax.pmax(jnp.max(logits, axis=-1), "vocab")
    exp_total, target_logit = lax.psum(
        (jnp.sum(jnp.exp(logits - row_peak[..., None]), axis=-1), local_target), "vocab"
    )
    log_total = row_peak + jnp.log(exp_total)
    token_loss = log_total - target_logit + zloss_weight * log_total * log_total
    mean_loss = lax.psum(jnp.sum(token_loss), ("dp", "seq")) / (
        examples * lax.axis_size("dp") * all_targets
    )
    logit_grad = (
        jnp.exp(logits - log_total[..., None]) * (1.0 + 2.0 * zloss_weight * log_total)[..., None]
        - target_hit.astype(jnp.float32)
    ).astype(jnp.bfloat16)
    grad_piece = lax.all_gather(logit_grad, "seq", axis=0, tiled=True)
    row_block = normed
    weight_acc = jnp.einsum(
        "tbd,tbv->dv", row_block, grad_piece, preferred_element_type=jnp.float32
    )
    hidden_part = jnp.einsum(
        "tbv,dv->tbd", grad_piece, head_weight, preferred_element_type=jnp.float32
    )
    head_total = lax.psum(weight_acc.astype(jnp.bfloat16), "dp")
    summed_grad = lax.psum(hidden_part, "vocab")
    gated = summed_grad * norm_gain
    dot_row = lax.psum(jnp.sum(gated * mixed_rows, axis=-1), "seq")
    mixed_grad = (
        gated * inverse_rms[..., None] - mixed_rows * (inverse_rms**3 * dot_row / D)[..., None]
    ).astype(jnp.bfloat16)
    row_block = mixed_grad
    attended_grad = lax.psum_scatter(
        jnp.einsum("tbd,fd->tbf", row_block, out_proj, preferred_element_type=jnp.float32),
        "seq",
        scatter_dimension=0,
        tiled=True,
    ).astype(jnp.bfloat16)
    grad_heads = attended_grad.reshape(tgt_rows, examples, heads_here, HDIM)
    prob_grad = jnp.einsum(
        "tbhd,bjhd->bhtj", grad_heads, value_heads, preferred_element_type=jnp.float32
    )
    score_grad = weights_full * (
        prob_grad - jnp.sum(weights_full * prob_grad, axis=-1, keepdims=True)
    )
    score_half = (score_grad * score_scale).astype(jnp.bfloat16)
    value_part = jnp.einsum(
        "bhtj,tbhd->bjhd", weights_half, grad_heads, preferred_element_type=jnp.float32
    )
    key_part = jnp.einsum(
        "bhtj,bthd->bjhd", score_half, query_heads, preferred_element_type=jnp.float32
    )
    key_grad, value_grad = (
        lax.psum_scatter(
            key_part.reshape(examples, enc_rows, features).astype(jnp.bfloat16),
            "seq",
            scatter_dimension=1,
            tiled=True,
        ).astype(jnp.float32),
        lax.psum_scatter(
            value_part.reshape(examples, enc_rows, features).astype(jnp.bfloat16),
            "seq",
            scatter_dimension=1,
            tiled=True,
        ).astype(jnp.float32),
    )
    return (mean_loss, head_total, key_grad, value_grad)


def solution(mesh):
    placed = (
        P("dp", "seq", "vocab"),
        P("dp", "seq", "vocab"),
        P("dp", "seq", "vocab"),
        P("dp"),
        P("vocab", "seq"),
        P("dp", None, "seq"),
        P("seq"),
        P("seq", "vocab"),
        P("dp", "seq"),
    )
    return jax.shard_map(
        body,
        mesh=mesh,
        in_specs=placed,
        out_specs=(P(), P("seq", "vocab"), P("dp", "seq", "vocab"), P("dp", "seq", "vocab")),
        check_vma=False,
    )
```

profile of v0, /device:TPU:1, one launch (start us, length us, event | category | flops | bytes accessed | tf_op | source)
XLA Modules:
  0.0 880.7 jit_solution(10574764354764928775)
XLA Ops:
  7.2 0.0 copy-start
  7.2 0.0 copy-start.5
  7.2 0.0 all-reduce.7.cloned.1.call-start
  7.2 22.1 %all_gather.12 = bf16[1,1024,256]{2,1,0:T(8,128)(2,1)S(1)} all-gather(bf16[1,128,256]{2,1,0:T(8,128)(2,1)} %param.10), channel_id=1, replica_groups=mesh['dp'=4,'seq'=8,'vocab'=16] {'seq'}, dimensions={1}, use_global_device_ids=true | all-gather | bytes 589824 | tf_op jit(solution)/shard_map/all_gather | solution.py:23
  30.0 19.8 %all_gather.13 = bf16[1,1024,256]{2,1,0:T(8,128)(2,1)S(1)} all-gather(bf16[1,128,256]{2,1,0:T(8,128)(2,1)} %param.11), channel_id=1, replica_groups=mesh['dp'=4,'seq'=8,'vocab'=16] {'seq'}, dimensions={1}, use_global_device_ids=true | all-gather | bytes 589824 | tf_op jit(solution)/shard_map/all_gather | solution.py:24
  49.8 1.1 fusion.42
  51.0 0.2 fusion.21
  51.2 0.0 copy-done.6
  51.2 0.2 fusion.3
  51.5 18.9 %all-gather = bf16[256,1,1,256]{3,0,2,1:T(8,128)(2,1)S(1)} all-gather(bf16[32,1,1,256]{3,0,2,1:T(8,128)(2,1)S(1)} %fusion.3), channel_id=2, replica_groups=mesh['dp'=4,'seq'=8,'vocab'=16] {'seq'}, dimensions={0}, use_global_device_ids=true | all-gather | bytes 147456 | tf_op jit(solution)/shard_map/all_gather | solution.py:44
  70.4 1.0 convolution_bitcast_fusion.2
  71.4 0.0 all-reduce.7.cloned.1.call-update
  71.4 0.0 all-reduce.13.cloned.1.call-start
  71.5 182.3 %all-reduce.7.cloned.1.call-done = f32[256,1,512]{2,0,1:T(8,128)} async-done(((f32[256,1,512]{2,0,1:T(8,128)}), f32[256,1,512]{2,0,1:T(8,128)}) %all-reduce.7.cloned.1.call-update) | async-done | bytes 524304 | tf_op jit(solution)/shard_map/psum | solution.py:48
  253.8 1.2 multiply_reduce_fusion.1
  255.0 13.7 %psum.57 = f32[256,1]{0,1:T(1,128)S(1)} all-reduce(f32[256,1]{0,1:T(1,128)S(1)} %bitcast.113), channel_id=1, replica_groups=mesh['dp'=4,'seq'=8,'vocab'=16] {'seq'}, use_global_device_ids=true, to_apply=%region_4.5 | all-reduce | flops 256 | bytes 2048 | tf_op jit(solution)/shard_map/psum | solution.py:49
  268.7 0.0 copy-done.9
  268.7 1.2 fusion.13
  269.9 2.0 convolution_bitcast_fusion
  271.9 6.1 copy.18
  278.0 0.0 all-reduce.13.cloned.1.call-update
  278.1 0.0 all-reduce.11.cloned.1.call-start
  278.1 1.3 dynamic-slice
  280.1 92.1 %all-reduce.13.cloned.1.call-done = f32[256,1,2008]{2,1,0:T(1,128)} async-done(((f32[256,1,2008]{2,1,0:T(1,128)}), f32[256,1,2008]{2,1,0:T(1,128)}) %all-reduce.13.cloned.1.call-update) | async-done | bytes 2056208
  372.2 1.3 fusion.41
  373.6 38.9 %pmax.7 = f32[32,1]{0,1:T(1,128)S(1)} all-reduce(f32[32,1]{0,1:T(1,128)S(1)} %bitcast.120), channel_id=1, replica_groups=mesh['dp'=4,'seq'=8,'vocab'=16] {'vocab'}, use_global_device_ids=true, to_apply=%region_7.8 | all-reduce | flops 32 | bytes 256 | tf_op jit(solution)/shard_map/pmax | solution.py:65
  412.5 0.6 exponential_reduce_fusion
  413.0 0.2 fusion.10
  413.2 32.1 %all-reduce.1 = (f32[32,1]{0,1:T(1,128)S(1)}, f32[32,1]{0,1:T(1,128)S(1)}) all-reduce(f32[32,1]{0,1:T(1,128)S(1)} %bitcast.118, f32[32,1]{0,1:T(1,128)S(1)} %bitcast.119), channel_id=1, replica_groups=mesh['dp'=4,'seq'=8,'vocab'=16] {'vocab'}, use_global_device_ids=true, to_apply=%region_9.10 | all-reduce | flops 64 | bytes 512 | tf_op jit(solution)/shard_map/psum | solution.py:66
  445.3 0.6 fusion.37
  446.0 0.2 fusion.12
  446.1 20.6 %all_gather.15 = bf16[256,1,2008]{2,0,1:T(8,128)(2,1)S(1)} all-gather(bf16[32,1,2008]{2,0,1:T(8,128)(2,1)S(1)} %fusion.12), channel_id=1, replica_groups=mesh['dp'=4,'seq'=8,'vocab'=16] {'seq'}, dimensions={0}, use_global_device_ids=true | all-gather | bytes 1156608 | tf_op jit(solution)/shard_map/all_gather | solution.py:78
  466.7 1.0 copy-done.2
  467.7 1.5 convolution_bitcast_fusion.1
  469.2 0.0 all-reduce.11.cloned.1.call-update
  469.3 0.0 reduce-scatter.6.cloned.1.call-start
  469.3 178.2 %all-reduce.11.cloned.1.call-done = f32[256,1,512]{2,0,1:T(8,128)} async-done(((f32[256,1,512]{2,0,1:T(8,128)}), f32[256,1,512]{2,0,1:T(8,128)}) %all-reduce.11.cloned.1.call-update) | async-done | bytes 524304 | tf_op jit(solution)/shard_map/psum | solution.py:87
  647.5 1.2 multiply_reduce_fusion
  648.8 13.7 %psum.63 = f32[256,1]{0,1:T(1,128)S(1)} all-reduce(f32[256,1]{0,1:T(1,128)S(1)} %bitcast.114), channel_id=1, replica_groups=mesh['dp'=4,'seq'=8,'vocab'=16] {'seq'}, use_global_device_ids=true, to_apply=%region_17.18 | all-reduce | flops 256 | bytes 2048 | tf_op jit(solution)/shard_map/psum | solution.py:89
  662.5 2.1 convolution_bitcast_fusion.3
  664.5 0.0 reduce-scatter.6.cloned.1.call-update
  664.5 0.0 reduce-scatter.10.cloned.1.call-start
  664.6 43.5 %reduce-scatter.6.cloned.1.call-done = f32[32,1,256]{2,0,1:T(8,128)} async-done(((f32[256,1,256]{2,0,1:T(8,128)}), f32[32,1,256]{2,0,1:T(8,128)}) %reduce-scatter.6.cloned.1.call-update) | async-done | bytes 32784 | tf_op jit(solution)/shard_map/reduce_scatter | solution.py:94
  708.1 1.2 fusion.1
  709.3 0.0 copy-start.7
  709.3 2.0 copy.22
  711.3 2.2 copy.28
  713.5 0.0 reduce-scatter.10.cloned.1.call-update
  713.5 0.0 reduce-scatter.8.cloned.1.call-start
  713.6 1.4 multiply_reduce_fusion.2
  715.0 1.2 fusion
  716.2 0.0 reduce-scatter.8.cloned.1.call-update
  716.2 0.0 all-reduce.9.cloned.1.call-start
  716.3 2.0 convolution_convert_fusion
  718.4 0.0 all-reduce.9.cloned.1.call-update
  718.4 60.4 %psum.60 = f32[]{:T(128)} all-reduce(f32[]{:T(128)} %get-tuple-element.26), channel_id=1, replica_groups=mesh['dp'=4,'seq'=8,'vocab'=16] {'dp','seq'}, use_global_device_ids=true, to_apply=%region_13.14 | all-reduce | flops 1 | bytes 8 | tf_op jit(solution)/shard_map/psum | solution.py:71
  779.4 0.0 reduce-scatter.10.cloned.1.call-done
  779.4 0.9 reshape_bitcast_fusion
  780.4 0.1 copy.23
  780.5 0.8 copy.21
  781.3 13.0 %reduce-scatter.8.cloned.1.call-done = bf16[1,128,256]{2,1,0:T(8,128)(2,1)} async-done(((bf16[1,1024,256]{2,1,0:T(8,128)(2,1)}), bf16[1,128,256]{2,1,0:T(8,128)(2,1)}) %reduce-scatter.8.cloned.1.call-update) | async-done | bytes 65552 | tf_op jit(solution)/shard_map/reduce_scatter | solution.py:115
  794.3 1.5 convert_element_type.128
  795.8 74.0 %all-reduce.9.cloned.1.call-done = bf16[512,2008]{0,1:T(8,128)(2,1)} async-done(((bf16[512,2008]{0,1:T(8,128)(2,1)}), bf16[512,2008]{0,1:T(8,128)(2,1)}) %all-reduce.9.cloned.1.call-update) | async-done | bytes 2056208 | tf_op jit(solution)/shard_map/psum | solution.py:86
  869.7 3.0 copy.34
  (20 shorter events, 0.1 us)
Async XLA Ops:
  7.2 262.7 %copy-start = (bf16[512,2008]{0,1:T(8,128)(2,1)S(1)}, bf16[512,2008]{0,1:T(8,128)(2,1)}, u32[]{:S(2)}) copy-start(bf16[512,2008]{0,1:T(8,128)(2,1)} %param.16) | copy-start | bytes 6168580
  7.2 63.2 %copy-start.5 = (bf16[256,512]{1,0:T(8,128)(2,1)S(1)}, bf16[256,512]{1,0:T(8,128)(2,1)}, u32[]{:S(2)}) copy-start(bf16[256,512]{1,0:T(8,128)(2,1)} %param.13) | copy-start | bytes 786436
  7.2 246.6 %all-reduce.7.cloned.1.call-start = ((), (), s32[]{:S(2)}) async-start(), calls=%async_computation.3 | async-start | bytes 1048576 | tf_op jit(solution)/shard_map/psum | solution.py:48
  29.3 224.5 %copy-start.4 = (bf16[1,256,512]{2,1,0:T(8,128)(2,1)S(1)}, bf16[1,256,512]{2,1,0:T(8,128)(2,1)}, u32[]{:S(2)}) copy-start(bf16[1,256,512]{2,1,0:T(8,128)(2,1)} %param.14) | copy-start | bytes 786436
  49.8 1.4 copy-start.6
  49.8 218.9 %copy-start.9 = (f32[512]{0:T(512)S(1)}, f32[512]{0:T(512)}, u32[]{:S(2)}) copy-start(f32[512]{0:T(512)} %param.15) | copy-start | bytes 6148
  71.4 300.8 %all-reduce.13.cloned.1.call-start = ((), (), s32[]{:S(2)}) async-start(), calls=%async_computation.9 | async-start | bytes 4194304
  278.0 135.0 %copy-start.10 = (s32[1,32]{1,0:T(1,128)S(1)}, s32[1,32]{1,0:T(1,128)}, u32[]{:S(2)}) copy-start(s32[1,32]{1,0:T(1,128)} %param.17) | copy-start | bytes 388
  278.1 369.5 %all-reduce.11.cloned.1.call-start = ((), (), s32[]{:S(2)}) async-start(), calls=%async_computation.5 | async-start | bytes 1048576 | tf_op jit(solution)/shard_map/psum | solution.py:87
  466.7 1.0 copy-start.2
  467.7 179.8 %copy-start.1 = (f32[256,1,512]{2,0,1:T(8,128)S(1)}, f32[256,1,512]{2,0,1:T(8,128)}, u32[]{:S(2)}) copy-start(f32[256,1,512]{2,0,1:T(8,128)} %all-reduce.7.cloned.1.call-done) | copy-start | bytes 1572868
  469.3 238.8 %reduce-scatter.6.cloned.1.call-start = ((), (), s32[]{:S(2)}) async-start(), calls=%async_computation.6 | async-start | bytes 294912 | tf_op jit(solution)/shard_map/reduce_scatter | solution.py:94
  664.5 114.9 %reduce-scatter.10.cloned.1.call-start = ((), (), s32[]{:S(2)}) async-start(), calls=%async_computation.8 | async-start | bytes 589824
  708.1 5.5 copy-start.8
  709.3 5.7 copy-start.7
  711.3 5.0 copy-start.3
  713.5 80.8 %reduce-scatter.8.cloned.1.call-start = ((), (), s32[]{:S(2)}) async-start(), calls=%async_computation.7 | async-start | bytes 589824 | tf_op jit(solution)/shard_map/reduce_scatter | solution.py:115
  716.2 153.5 %all-reduce.9.cloned.1.call-start = ((), (), s32[]{:S(2)}) async-start(), calls=%async_computation.4 | async-start | bytes 4112384 | tf_op jit(solution)/shard_map/psum | solution.py:86
Sparse Core Ops, SparseCore 0:
  71.6 182.1 all-reduce.6
  278.2 93.9 all-reduce.12
  469.4 178.1 all-reduce.10
  664.7 43.3 reduce-scatter.5
  713.6 39.4 reduce-scatter.9
  755.8 38.4 reduce-scatter.7
  798.1 71.5 all-reduce.8
where the time goes:
time: 882 us; the launch traced here: 881 us
  waiting for transfers between devices  583 us (66%)
  blocking collectives  240 us (27%)
  local copies, waits for them, and re-layouts  17.4 us (2%)
  between operations  17.4 us (2%)
  matrix products  13.9 us (2%)
    psum x1, waiting for transfers between devices, body(): lax.psum(mixed_part, 'vocab')  182 us
    psum x1, waiting for transfers between devices, body(): summed_grad = lax.psum(hidden_part, 'vocab')  178 us
    unnamed x9, waiting for transfers between devices  92.3 us
    psum x1, waiting for transfers between devices, body(): head_total = lax.psum(weight_acc.astype(jnp.bfloat16), 'dp')  74 us
    psum x1, blocking collectives, body(): lax.psum(jnp.sum(token_loss), ('dp', 'seq'))  60.4 us
    reduce_scatter x1, waiting for transfers between devices, body(): lax.psum_scatter(jnp.einsum('tbd,fd->tbf', row_block, out_proj, preferred...  43.5 us
    pmax x1, blocking collectives, body(): row_peak = lax.pmax(jnp.max(logits, axis=-1), 'vocab')  38.9 us
    psum x1, blocking collectives, body(): lax.psum((jnp.sum(jnp.exp(logits - row_peak[..., None]), axis=-1), local_...  32.1 us
  transfers between devices with their start and end apart: 7, of which 6 were waited for; matrix products, arithmetic and copies ran while one was open for 1% of the time, Pallas kernels for 0%

commit v1 on v0

v1 whole, which is shorter than its diff:
```python
import functools
import types

import jax
import jax.numpy as jnp
from jax import lax
from jax.experimental import pallas as pl
from jax.experimental.pallas import tpu as pltpu
from jax.sharding import PartitionSpec as P

HDIM = 256
ZW = 0.0001
EPS = 1e-06
MESH = pl.DeviceIdType.MESH
F32 = jnp.float32
BF16 = jnp.bfloat16


def dot(a, b, ca, cb):
    return lax.dot_general(a, b, (((ca,), (cb,)), ((), ())), preferred_element_type=F32)


def eye(n, m):
    return lax.broadcasted_iota(jnp.int32, (n, m), 0) == lax.broadcasted_iota(jnp.int32, (n, m), 1)


def to_row(col, n):
    return jnp.sum(jnp.where(eye(n, 128), jnp.broadcast_to(col, (n, 128)), 0.0), axis=0, keepdims=True)


def to_col(row, n):
    return jnp.sum(jnp.where(eye(n, 128), jnp.broadcast_to(row, (n, 128)), 0.0), axis=1, keepdims=True)


def lane_pick(first, second, n):
    lane = lax.broadcasted_iota(jnp.int32, (n, 128), 1)
    return jnp.where(lane < 64, first, second)


def sub_pick(rows):
    sub = lax.broadcasted_iota(jnp.int32, (8, 128), 0)
    tile = jnp.zeros((8, 128), F32)
    for i, row in enumerate(rows):
        tile = jnp.where(sub == i, row, tile)
    return tile


def kernel(cfg, q, k, v, ln, wo, res, gain, w_hbm, tgt, out_loss, out_hg, out_kg, out_vg, *scratch):
    NS, NV, TR, KJ, C, V, VP, batch_rows = cfg
    b = types.SimpleNamespace(**dict(zip(scratch_list(cfg), scratch)))
    HD = HDIM
    R = TR * NS
    RB = R // NV
    NB = TR // RB
    H = NS // 2
    VH = VP // 2
    D = C * NS
    scale = HD ** (-0.5)
    md, ms, mv = lax.axis_index("dp"), lax.axis_index("seq"), lax.axis_index("vocab")
    core = lax.rem(md, 2)
    zlo = md // 2
    mate = md + 1 - 2 * core
    zmate = lax.rem(md + 2, 4)
    right, left = lax.rem(ms + 1, NS), lax.rem(ms + NS - 1, NS)
    ssem, rsem = b.ssem, b.rsem
    used = [0]

    def sem():
        used[0] += 1
        return ssem.at[used[0] - 1], rsem.at[used[0] - 1]

    def push(src, dst, axis, to, sems):
        copy = pltpu.make_async_remote_copy(
            src_ref=src, dst_ref=dst, send_sem=sems[0], recv_sem=sems[1],
            device_id={axis: to}, device_id_type=MESH)
        copy.start()
        return copy

    drains = []

    def wait_bytes(ref, one):
        pltpu.make_async_copy(ref, ref, one).wait()

    def spread(src, dst, axis):
        me, n = (ms, NS) if axis == "seq" else (mv, NV)
        sems = sem()
        for step in range(1, n):
            push(src, dst.at[me], axis, lax.rem(me + step, n), sems)
        rest = dst.at[pl.ds(0, n - 1)]
        drains.append((rest, sems[0]))
        return lambda: wait_bytes(rest, sems[1])

    def scatter(src, dst, axis):
        me, n = (ms, NS) if axis == "seq" else (mv, NV)
        sems = sem()
        for step in range(1, n):
            to = lax.rem(me + step, n)
            push(src.at[to], dst.at[step - 1], axis, to, sems)
        rest = dst.at[pl.ds(0, n - 1)]
        drains.append((rest, sems[0]))
        return lambda: wait_bytes(rest, sems[1])

    def one(src, dst, axis, to):
        copy = push(src, dst, axis, to, sem())
        drains.append(copy)
        return copy.wait_recv

    barrier = pltpu.get_barrier_semaphore()
    for step in range(1, NS):
        pl.semaphore_signal(barrier, inc=1, device_id={"seq": lax.rem(ms + step, NS)}, device_id_type=MESH)
    for step in range(1, NV):
        pl.semaphore_signal(barrier, inc=1, device_id={"vocab": lax.rem(mv + step, NV)}, device_id_type=MESH)
    for to in (mate, zmate):
        pl.semaphore_signal(barrier, inc=1, device_id={"dp": to}, device_id_type=MESH)
    w_copy = pltpu.make_async_copy(w_hbm, b.w_in, b.lsem.at[0])
    w_copy.start()
    pl.semaphore_wait(barrier, NS - 1 + NV - 1 + 2)

    got_q = spread(q, b.q_all, "seq")
    b.q_all[ms] = q[...]
    w_copy.wait()
    w = b.w
    tail = V // 128 * 128
    w[:, 0:tail] = b.w_in[:, 0:tail]
    if tail < VP:
        w[:, tail:VP] = jnp.zeros((C, VP - tail), BF16)
        w[:, tail:V] = b.w_in[:, tail:V]
    got_q()
    q_rows = b.q_all[...].reshape(R, HD)
    s = dot(q_rows, k[...], 1, 1) * scale
    place = lax.broadcasted_iota(jnp.int32, (R, KJ), 1) + ms * KJ
    s = jnp.where(place < ln[0], s, -jnp.inf)
    b.s[...] = s
    peak = jnp.maximum(jnp.max(s, axis=1, keepdims=True), -1e30)
    e = jnp.exp(s - peak)
    total = jnp.sum(e, axis=1, keepdims=True)
    acc = dot(e.astype(BF16), v[...], 1, 0) / jnp.maximum(total, 1e-30)
    b.acc_send[...] = acc.astype(BF16).reshape(NS, TR, HD)
    b.st_send[...] = lane_pick(peak, total, R).reshape(NS, TR, 128)
    got_st = scatter(b.st_send, b.st_recv, "seq")
    got_acc = scatter(b.acc_send, b.acc_recv, "seq")
    got_st()
    tiles = [b.st_send[ms]] + [b.st_recv[i] for i in range(NS - 1)]
    peaks = [t[:, 0:1] for t in tiles]
    totals = [t[:, 64:65] for t in tiles]
    top = functools.reduce(jnp.maximum, peaks)
    parts = [t * jnp.exp(p - top) for t, p in zip(totals, peaks)]
    whole = functools.reduce(jnp.add, parts)
    got_acc()
    accs = [b.acc_send[ms]] + [b.acc_recv[i] for i in range(NS - 1)]
    att = functools.reduce(jnp.add, [a.astype(F32) * (p / whole) for a, p in zip(accs, parts)])
    b.att_all[ms] = att.astype(BF16)
    b.stat_all[ms] = lane_pick(top, whole, TR)
    got_att = spread(b.att_all.at[ms], b.att_all, "seq")
    got_stat = spread(b.stat_all.at[ms], b.stat_all, "seq")
    got_att()

    mixed_part = dot(b.att_all[...].reshape(R, HD), wo[...], 1, 0)
    b.mix_send[...] = mixed_part.astype(BF16).reshape(NV, RB, C)
    got_mix = scatter(b.mix_send, b.mix_recv, "vocab")
    mine = res[pl.ds(pl.multiple_of(mv * RB, RB), RB), :].astype(F32)
    got_mix()
    mixed = mine + b.mix_send[mv].astype(F32)
    for i in range(NV - 1):
        mixed = mixed + b.mix_recv[i].astype(F32)
    b.mixed[...] = mixed
    b.mg[mv] = (mixed * gain[...]).astype(BF16)
    got_mg = spread(b.mg.at[mv], b.mg, "vocab")
    b.sq[ms] = sub_pick([to_row(jnp.sum(mixed * mixed, axis=1, keepdims=True), RB)])
    got_sq = spread(b.sq.at[ms], b.sq, "seq")
    got_sq()
    square = jnp.sum(b.sq[...], axis=0)[0:1]
    b.inv[mv] = sub_pick([lax.rsqrt(square / D + EPS)])
    got_inv = spread(b.inv.at[mv], b.inv, "vocab")
    got_mg()

    def rows_of(owner):
        return b.mg[pl.ds(owner * NB, NB)].reshape(TR, C)

    def at(distance):
        return lax.rem(ms + distance + NS, NS)

    half = [slice(0, VH), slice(VH, VP)]
    cw_send, cw_recv, cc_send, cc_recv = b.cw_send, b.cw_recv, b.cc_send, b.cc_recv
    cw_got, cc_got = {}, {}
    far = rows_of(at(H))
    for hh in range(2):
        block = dot(far, w[:, half[hh]], 1, 0)
        if hh == 0:
            cw_send[0, 0] = block
            cw_got[0, 0] = one(cw_send.at[0, 0], cw_recv.at[0, 0], "seq", right)
        else:
            cc_send[0, 1] = block
            cc_got[0, 1] = one(cc_send.at[0, 1], cc_recv.at[0, 1], "seq", left)
    for step in range(1, H):
        both = jnp.concatenate([rows_of(at(H - step)), rows_of(at(step - H))], axis=0)
        for hh in range(2):
            block = dot(both, w[:, half[hh]], 1, 0)
            cw_send[step, hh] = block[:TR]
            cc_send[step, hh] = block[TR:]
        for hh in range(2):
            for way in ((0, 1) if hh == 0 else (1, 0)):
                sends, recvs, got, to = ((cw_send, cw_recv, cw_got, right), (cc_send, cc_recv, cc_got, left))[way]
                if (step - 1, hh) in got:
                    got[step - 1, hh]()
                    sends[step, hh] = sends[step, hh] + recvs[step - 1, hh]
                got[step, hh] = one(sends.at[step, hh], recvs.at[step, hh], "seq", to)
    own = rows_of(ms)
    for hh in range(2):
        b.logits[:, half[hh]] = dot(own, w[:, half[hh]], 1, 0)
    got_inv()
    normed = []
    for i in range(NV):
        normed.append(b.mg[i].astype(F32) * to_col(b.inv[i][0:1], RB))
    b.normed_t[...] = jnp.transpose(jnp.concatenate(normed, axis=0)).astype(BF16)
    inv_own = jnp.concatenate([to_col(b.inv[ms * NB + i][0:1], RB) for i in range(NB)], axis=0)
    for hh in range(2):
        block = b.logits[:, half[hh]]
        for got, recvs in ((cw_got, cw_recv), (cc_got, cc_recv)):
            if (H - 1, hh) in got:
                got[H - 1, hh]()
                block = block + recvs[H - 1, hh]
        block = block * inv_own
        if hh == 1:
            col = lax.broadcasted_iota(jnp.int32, (TR, VH), 1) + VH
            block = jnp.where(col < V, block, -jnp.inf)
        b.logits[:, half[hh]] = block

    logits = b.logits[...]
    tgt_col = to_col(jnp.concatenate([tgt[...].astype(F32), jnp.zeros((1, 128 - TR), F32)], axis=1), TR)
    tgt_col = tgt_col.astype(jnp.int32) - mv * V
    col = lax.broadcasted_iota(jnp.int32, (TR, VP), 1)
    hit = jnp.logical_and(col == tgt_col, col < V)
    row_peak = jnp.max(logits, axis=1, keepdims=True)
    row_sum = jnp.sum(jnp.exp(logits - row_peak), axis=1, keepdims=True)
    row_tgt = jnp.sum(jnp.where(hit, logits, 0.0), axis=1, keepdims=True)
    b.stats[mv] = sub_pick([to_row(x, TR) for x in (row_peak, row_sum, row_tgt)])
    got_stats = spread(b.stats.at[mv], b.stats, "vocab")
    got_stats()
    st = b.stats[...]
    tops = jnp.max(st[:, 0:1, :], axis=0)
    sums = jnp.sum(st[:, 1:2, :] * jnp.exp(st[:, 0:1, :] - tops[None]), axis=0)
    hits = jnp.sum(st[:, 2:3, :], axis=0)
    log_total = tops + jnp.log(sums)
    loss = log_total - hits + ZW * log_total * log_total
    lane = lax.broadcasted_iota(jnp.int32, (1, 128), 1)
    loss = jnp.where(lane < TR, loss, 0.0)
    lt = to_col(jnp.where(lane < TR, log_total, 0.0), TR)
    grad = jnp.exp(logits - lt) * (1.0 + 2.0 * ZW * lt) - hit.astype(F32)
    grad = grad.astype(BF16)
    g_all = b.g_all
    for hh in range(2):
        g_all[ms, hh] = grad[:, half[hh]]

    cw_got, cc_got = {}, {}

    def forward(step, hh, way):
        if step == H - 1 and hh != way:
            return
        got, to, owner = ((cw_got, right, at(-step)), (cc_got, left, at(step)))[way]
        if step > 0:
            got[step - 1, hh]()
        got[step, hh] = one(g_all.at[owner, hh], g_all.at[owner, hh], "seq", to)

    def hidden(owners):
        out = None
        for hh in range(2):
            rows = jnp.concatenate([g_all[o, hh] for o in owners], axis=0)
            term = dot(rows, w[:, half[hh]], 1, 1)
            out = term if out is None else out + term
        out = out.astype(BF16)
        for i, o in enumerate(owners):
            b.hid_send[pl.ds(o * NB, NB)] = out[i * TR:(i + 1) * TR].reshape(NB, RB, C)

    for step in range(H):
        for hh in range(2):
            for way in range(2):
                forward(step, hh, way)
        if step == 0:
            b.loss[ms] = sub_pick([loss])
            got_loss = spread(b.loss.at[ms], b.loss, "seq")
            hidden([ms])
        else:
            for got in (cw_got, cc_got):
                for hh in range(2):
                    if step == H - 1 and (step, hh) not in got:
                        got[step - 1, hh]()
            hidden([at(-step), at(step)])
    cw_got[H - 1, 0]()
    cc_got[H - 1, 1]()
    hidden([at(H)])
    got_hid = scatter(b.hid_send, b.hid_recv, "vocab")

    QC = C // 4

    def head(start, size):
        rows = b.normed_t[pl.ds(pl.multiple_of(start, QC), size), :]
        return [dot(rows, g_all[:, hh].reshape(R, VH), 1, 0).astype(BF16) for hh in range(2)]

    hp = 1 - core
    for i in range(2):
        for hh, block in enumerate(head((2 * hp + i) * QC, QC)):
            b.hg_send[i, :, half[hh]] = block
    got_h1 = one(b.hg_send, b.hg_recv, "dp", mate)

    got_hid()
    normed_grad = b.hid_send[mv].astype(F32)
    for i in range(NV - 1):
        normed_grad = normed_grad + b.hid_recv[i].astype(F32)
    gated = normed_grad * gain[...]
    mixed = b.mixed[...]
    b.dots[ms] = sub_pick([to_row(jnp.sum(gated * mixed, axis=1, keepdims=True), RB)])
    got_dots = spread(b.dots.at[ms], b.dots, "seq")
    for i in range(2):
        for hh, block in enumerate(head((2 * core + i) * QC, QC)):
            b.hg_own[i, :, half[hh]] = block
    got_loss()
    b.loss1[0] = jnp.sum(b.loss[...], axis=0)
    got_l1 = one(b.loss1.at[0], b.loss1.at[1], "dp", mate)
    got_dots()
    dots = to_col(jnp.sum(b.dots[...], axis=0)[0:1], RB)
    inv = to_col(b.inv[mv][0:1], RB)
    mixed_grad = gated * inv - mixed * (inv * inv * inv * dots / D)
    b.mgrad[mv] = mixed_grad.astype(BF16)
    got_mgrad = spread(b.mgrad.at[mv], b.mgrad, "vocab")

    got_h1()
    zq = 1 - zlo
    b.q_send[...] = (b.hg_own[zq].astype(F32) + b.hg_recv[zq].astype(F32)).astype(BF16)
    got_h2 = one(b.q_send, b.q_recv, "dp", zmate)
    got_l1()
    b.loss2[0] = b.loss1[0] + b.loss1[1]
    got_l2 = one(b.loss2.at[0], b.loss2.at[1], "dp", zmate)

    got_mgrad()
    ag_part = dot(b.mgrad[...].reshape(R, C), wo[...], 1, 1)
    b.ag_send[...] = ag_part.astype(BF16).reshape(NS, TR, HD)
    got_ag = scatter(b.ag_send, b.ag_recv, "seq")
    got_stat()
    stat = b.stat_all[...].reshape(R, 128)
    weights = jnp.exp(b.s[...] - stat[:, 0:1]) / stat[:, 64:65]
    weights_half = weights.astype(BF16)
    got_ag()
    ag = b.ag_send[ms].astype(F32)
    for i in range(NS - 1):
        ag = ag + b.ag_recv[i].astype(F32)
    b.ag_all[ms] = ag.astype(BF16)
    got_ag_all = spread(b.ag_all.at[ms], b.ag_all, "seq")
    got_ag_all()
    ag_rows = b.ag_all[...].reshape(R, HD)
    prob_grad = dot(ag_rows, v[...], 1, 1)
    delta = jnp.sum(weights * prob_grad, axis=1, keepdims=True)
    step = min(R, 128)
    for i in range(R // step):
        b.delta[ms, i] = sub_pick([to_row(delta[i * step:(i + 1) * step], step)])
    got_delta = spread(b.delta.at[ms], b.delta, "seq")
    out_vg[...] = dot(weights_half, ag_rows, 0, 0)
    got_delta()
    deltas = jnp.sum(b.delta[...], axis=0)
    delta = jnp.concatenate([to_col(deltas[i, 0:1], step) for i in range(R // step)], axis=0)
    score_grad = (weights * (prob_grad - delta) * scale).astype(BF16)
    out_kg[...] = dot(score_grad, b.q_all[...].reshape(R, HD), 0, 0)

    got_h2()
    fin = b.fin
    mine_at = 2 * core + zlo
    fin[mine_at] = (
        b.hg_own[zlo].astype(F32) + b.hg_recv[zlo].astype(F32) + b.q_recv[...].astype(F32)
    ).astype(BF16)
    got_f1 = one(fin.at[mine_at], fin.at[mine_at], "dp", zmate)
    got_f2 = one(fin.at[mine_at], fin.at[mine_at], "dp", mate)
    got_l2()
    loss = (b.loss2[0] + b.loss2[1])[0:1]
    out_loss[...] = jnp.sum(loss, axis=1, keepdims=True) / batch_rows
    got_f1()
    other_at = 2 * core + zq
    got_f3 = one(fin.at[other_at], fin.at[other_at], "dp", mate)
    got_f2()
    got_f3()
    store = pltpu.make_async_copy(fin, out_hg, b.lsem.at[1])
    store.start()
    for item in drains:
        if isinstance(item, tuple):
            wait_bytes(*item)
        else:
            item.wait_send()
    store.wait()


def scratch_list(cfg):
    NS, NV, TR, KJ, C, V, VP, batch_rows = cfg
    HD = HDIM
    R = TR * NS
    RB = R // NV
    H = NS // 2
    VH = VP // 2
    blocks = max(1, R // 128)

    def vm(*shape, dtype=BF16):
        return pltpu.VMEM(shape, dtype)

    return dict(
        w_in=vm(C, V), w=vm(C, VP),
        q_all=vm(NS, TR, HD), s=vm(R, KJ, dtype=F32),
        acc_send=vm(NS, TR, HD), acc_recv=vm(NS, TR, HD),
        st_send=vm(NS, TR, 128, dtype=F32), st_recv=vm(NS, TR, 128, dtype=F32),
        att_all=vm(NS, TR, HD), stat_all=vm(NS, TR, 128, dtype=F32),
        mix_send=vm(NV, RB, C), mix_recv=vm(NV, RB, C), mixed=vm(RB, C, dtype=F32),
        mg=vm(NV, RB, C), sq=vm(NS, 8, 128, dtype=F32), inv=vm(NV, 8, 128, dtype=F32),
        cw_send=vm(H, 2, TR, VH, dtype=F32), cw_recv=vm(H, 2, TR, VH, dtype=F32),
        cc_send=vm(H, 2, TR, VH, dtype=F32), cc_recv=vm(H, 2, TR, VH, dtype=F32),
        logits=vm(TR, VP, dtype=F32), stats=vm(NV, 8, 128, dtype=F32),
        normed_t=vm(C, R), g_all=vm(NS, 2, TR, VH),
        loss=vm(NS, 8, 128, dtype=F32), loss1=vm(2, 8, 128, dtype=F32),
        loss2=vm(2, 8, 128, dtype=F32),
        hid_send=vm(NV, RB, C), hid_recv=vm(NV, RB, C), dots=vm(NS, 8, 128, dtype=F32),
        mgrad=vm(NV, RB, C), ag_send=vm(NS, TR, HD), ag_recv=vm(NS, TR, HD),
        ag_all=vm(NS, TR, HD), delta=vm(NS, blocks, 8, 128, dtype=F32),
        hg_send=vm(2, C // 4, VP), hg_recv=vm(2, C // 4, VP), hg_own=vm(2, C // 4, VP),
        q_send=vm(C // 4, VP), q_recv=vm(C // 4, VP), fin=vm(4, C // 4, VP),
        ssem=pltpu.SemaphoreType.DMA((80,)), rsem=pltpu.SemaphoreType.DMA((80,)),
        lsem=pltpu.SemaphoreType.DMA((2,)),
    )


def body(sizes, queries, enc_keys, enc_values, enc_lengths, out_proj, residual, norm_gain, head_weight, targets):
    ND, NS, NV = sizes
    TR = queries.shape[1]
    KJ = enc_keys.shape[1]
    C, V = head_weight.shape
    VP = (V + 255) // 256 * 256
    cfg = (NS, NV, TR, KJ, C, V, VP, ND * TR * NS)
    vmem = pl.BlockSpec(memory_space=pltpu.VMEM)
    call = pl.pallas_call(
        functools.partial(kernel, cfg),
        out_shape=(
            jax.ShapeDtypeStruct((1, 1), F32),
            jax.ShapeDtypeStruct((4, C // 4, VP), BF16),
            jax.ShapeDtypeStruct((KJ, HDIM), F32),
            jax.ShapeDtypeStruct((KJ, HDIM), F32),
        ),
        in_specs=[vmem, vmem, vmem, pl.BlockSpec(memory_space=pltpu.SMEM), vmem, vmem, vmem,
                  pl.BlockSpec(memory_space=pl.ANY), vmem],
        out_specs=(vmem, pl.BlockSpec(memory_space=pl.ANY), vmem, vmem),
        scratch_shapes=list(scratch_list(cfg).values()),
        compiler_params=pltpu.CompilerParams(
            collective_id=0, has_side_effects=True, vmem_limit_bytes=48 * 1024 * 1024),
    )
    loss, hg, kg, vg = call(
        queries[0], enc_keys[0], enc_values[0], enc_lengths, out_proj, residual[0],
        norm_gain.reshape(1, C), head_weight, targets)
    return (loss.reshape(()), hg.reshape(C, VP)[:, :V], kg[None], vg[None])


def solution(mesh):
    placed = (
        P("dp", "seq", "vocab"),
        P("dp", "seq", "vocab"),
        P("dp", "seq", "vocab"),
        P("dp"),
        P("vocab", "seq"),
        P("dp", None, "seq"),
        P("seq"),
        P("seq", "vocab"),
        P("dp", "seq"),
    )
    sizes = (mesh.shape["dp"], mesh.shape["seq"], mesh.shape["vocab"])
    return jax.shard_map(
        functools.partial(body, sizes),
        mesh=mesh,
        in_specs=placed,
        out_specs=(P(), P("seq", "vocab"), P("dp", "seq", "vocab"), P("dp", "seq", "vocab")),
        check_vma=False,
    )
```

time: 882 us -> 161 us (0.18)
  waiting for transfers between devices: 583 us -> 0 us
  blocking collectives: 240 us -> 0 us
  Pallas kernels: 0 us -> 148 us
  between operations: 17.4 us -> 3.24 us
  matrix products: 13.9 us -> 0 us
    psum x3 -> x0, waiting for transfers between devices: 434 us -> none  [the longest x1 182 us: body(): lax.psum(mixed_part, 'vocab')]
    pallas_call x0 -> x1, Pallas kernels: none -> 148 us  [body(): call(queries[0], enc_keys[0], enc_values[0], enc_lengths, out_proj, resid...]
    psum x4 -> x0, blocking collectives: 120 us -> none  [the longest x1 60.4 us: body(): lax.psum(jnp.sum(token_loss), ('dp', 'seq'))]
    unnamed x9 -> x0, waiting for transfers between devices: 92.3 us -> none
    all_gather x4 -> x0, blocking collectives: 81.4 us -> none  [the longest x1 22.1 us: body(): lax.all_gather(enc_keys, 'seq', axis=1, tiled=True)]
    reduce_scatter x2 -> x0, waiting for transfers between devices: 56.5 us -> none  [the longest x1 43.5 us: body(): lax.psum_scatter(jnp.einsum('tbd,fd->tbf', row_block, out_proj, preferred...]
    pmax x1 -> x0, blocking collectives: 38.9 us -> none  [body(): row_peak = lax.pmax(jnp.max(logits, axis=-1), 'vocab')]
    dot_general x10 -> x0, matrix products: 13.9 us -> none  [the longest x1 2.06 us: body(): jnp.einsum('tbd,fd->tbf', row_block, out_proj, preferred_element_type=jnp...]
  transfers between devices with their start and end apart: 7 -> 0, of which waited for: 6 -> 0; matrix products, arithmetic and copies ran while one was open for 1% -> 0% of each run, Pallas kernels for 0% -> 0%
where the time goes in v1:
time: 161 us
  Pallas kernels  148 us (92%)
  local copies, waits for them, and re-layouts  9.5 us (6%)
  between operations  3.24 us (2%)
    pallas_call x1, Pallas kernels, body(): call(queries[0], enc_keys[0], enc_values[0], enc_lengths, out_proj, resid...  148 us
    unnamed x20, local copies, waits for them, and re-layouts  9.5 us

profile of v1, /device:TPU:1, one launch (start us, length us, event | category | flops | bytes accessed | tf_op | source)
XLA Modules:
  0.0 160.5 jit_solution(1889539380320935277)
XLA Ops:
  0.6 0.0 copy-start.7
  0.6 0.0 copy-start.6
  0.7 0.0 copy-start.2
  0.7 0.0 copy-start.1
  0.7 0.0 copy-start.4
  0.7 0.0 copy-start.3
  0.7 0.0 copy-start.5
  1.4 2.9 %copy.13.w_hbm = bf16[512,2008]{1,0:T(8,128)(2,1)S(1)} copy(bf16[512,2008]{0,1:T(8,128)(2,1)} %param.16) | data formatting | bytes 4112384 | tf_op args[7]
  4.3 0.0 copy-done.7
  4.3 0.0 copy-done.6
  4.4 0.0 copy-done.2
  4.4 0.0 copy-done.1
  4.4 0.0 copy-done.4
  4.4 0.0 copy-done.3
  4.4 0.0 copy-done.5
  4.4 147.8 %shard_map.120 = (f32[1,1]{1,0:T(1,128)}, bf16[4,128,2048]{2,1,0:T(8,128)(2,1)S(1)}, f32[128,256]{1,0:T(8,128)S(1)}, f32[128,256]{1,0:T(8,128)S(1)}) custom-call(bf16[32,256]{1,0:T(8,128)(2,1)S(1)} %bitcast.16, bf16[128,256]{1,0:T(8,128)(2,1)S(1)} %bitcast.14, bf16[128,256]{1,0:T(8,128)(2,1)S(1)} %bitcast.15, s32[1]{0:T(128)S(6)} %copy.19.ln, ...), custom_call_target="tpu_custom_call" | custom-call | tf_op jit(solution)/shard_map/pallas_call | solution.py:449
  152.2 0.0 copy-start
  152.2 1.3 copy-done
  153.6 3.9 %copy.15 = bf16[512,2008]{0,1:T(8,128)(2,1)} copy(bf16[512,2008]{1,0:T(8,128)(2,1)} %bitcast.10) | data formatting | bytes 4112384
  158.1 0.7 copy.21
  158.8 0.7 copy.22
Async XLA Ops:
  0.6 3.7 %copy-start.7 = (s32[1,32]{1,0:T(1,128)S(1)}, s32[1,32]{1,0:T(1,128)}, u32[]{:S(2)}) copy-start(s32[1,32]{1,0:T(1,128)} %tgt.1) | copy-start | bytes 388
  0.6 3.7 %copy-start.6 = (f32[512]{0:T(512)S(1)}, f32[512]{0:T(512)}, u32[]{:S(2)}) copy-start(f32[512]{0:T(512)} %param.15) | copy-start | bytes 6148
  0.7 3.7 %copy-start.2 = (bf16[1,256,512]{2,1,0:T(8,128)(2,1)S(1)}, bf16[1,256,512]{2,1,0:T(8,128)(2,1)}, u32[]{:S(2)}) copy-start(bf16[1,256,512]{2,1,0:T(8,128)(2,1)} %param.14) | copy-start | bytes 786436
  0.7 3.7 %copy-start.1 = (bf16[256,512]{1,0:T(8,128)(2,1)S(1)}, bf16[256,512]{1,0:T(8,128)(2,1)}, u32[]{:S(2)}) copy-start(bf16[256,512]{1,0:T(8,128)(2,1)} %wo.1) | copy-start | bytes 786436
  0.7 3.7 %copy-start.4 = (bf16[1,128,256]{2,1,0:T(8,128)(2,1)S(1)}, bf16[1,128,256]{2,1,0:T(8,128)(2,1)}, u32[]{:S(2)}) copy-start(bf16[1,128,256]{2,1,0:T(8,128)(2,1)} %param.11) | copy-start | bytes 196612
  0.7 3.7 %copy-start.3 = (bf16[1,128,256]{2,1,0:T(8,128)(2,1)S(1)}, bf16[1,128,256]{2,1,0:T(8,128)(2,1)}, u32[]{:S(2)}) copy-start(bf16[1,128,256]{2,1,0:T(8,128)(2,1)} %param.10) | copy-start | bytes 196612
  0.7 3.7 %copy-start.5 = (bf16[1,32,256]{2,1,0:T(8,128)(2,1)S(1)}, bf16[1,32,256]{2,1,0:T(8,128)(2,1)}, u32[]{:S(2)}) copy-start(bf16[1,32,256]{2,1,0:T(8,128)(2,1)} %param.9) | copy-start | bytes 49156
  152.2 1.3 copy-start

commit v2 on v1

v2 whole, which is shorter than its diff:
```python
import functools
import types

import jax
import jax.numpy as jnp
from jax import lax
from jax.experimental import pallas as pl
from jax.experimental.pallas import tpu as pltpu
from jax.sharding import PartitionSpec as P

HDIM = 256
ZW = 0.0001
EPS = 1e-06
MESH = pl.DeviceIdType.MESH
F32 = jnp.float32
BF16 = jnp.bfloat16


def dot(a, b, ca, cb):
    return lax.dot_general(a, b, (((ca,), (cb,)), ((), ())), preferred_element_type=F32)


def eye(n, m):
    return lax.broadcasted_iota(jnp.int32, (n, m), 0) == lax.broadcasted_iota(jnp.int32, (n, m), 1)


def to_row(col, n):
    return jnp.sum(jnp.where(eye(n, 128), jnp.broadcast_to(col, (n, 128)), 0.0), axis=0, keepdims=True)


def to_col(row, n):
    return jnp.sum(jnp.where(eye(n, 128), jnp.broadcast_to(row, (n, 128)), 0.0), axis=1, keepdims=True)


def sub_pick(rows):
    sub = lax.broadcasted_iota(jnp.int32, (8, 128), 0)
    tile = jnp.zeros((8, 128), F32)
    for i, row in enumerate(rows):
        tile = jnp.where(sub == i, row, tile)
    return tile


def kernel(cfg, q_hbm, k_hbm, v_hbm, ln, wo_hbm, res_hbm, gain_hbm, w_hbm, tgt_hbm, out_loss, out_hg, out_kg, out_vg, *scratch):
    NS, NV, TR, KJ, C, V, VP, batch_rows = cfg
    b = types.SimpleNamespace(**dict(zip(scratch_list(cfg), scratch)))
    HD = HDIM
    R = TR * NS
    RB = R // NV
    NB = TR // RB
    H = NS // 2
    VH = VP // 2
    D = C * NS
    scale = HD ** (-0.5)
    md, ms, mv = lax.axis_index("dp"), lax.axis_index("seq"), lax.axis_index("vocab")
    core = lax.rem(md, 2)
    zlo = md // 2
    mate = md + 1 - 2 * core
    zmate = lax.rem(md + 2, 4)
    right, left = lax.rem(ms + 1, NS), lax.rem(ms + NS - 1, NS)
    ssem, rsem = b.ssem, b.rsem
    used = [0]

    def sem():
        used[0] += 1
        return ssem.at[used[0] - 1], rsem.at[used[0] - 1]

    def push(src, dst, axis, to, sems):
        copy = pltpu.make_async_remote_copy(
            src_ref=src, dst_ref=dst, send_sem=sems[0], recv_sem=sems[1],
            device_id={axis: to}, device_id_type=MESH)
        copy.start()
        return copy

    drains = []

    def wait_bytes(ref, one):
        pltpu.make_async_copy(ref, ref, one).wait()

    NX = min(4, NV)
    NZ = NV // NX
    vx, vz = lax.rem(mv, NX), mv // NX
    seq_steps = sorted(range(1, NS), key=lambda a: -min(a, NS - a))
    vocab_steps = sorted(
        [(a, c) for a in range(NZ) for c in range(NX) if a or c],
        key=lambda d: -(2 * min(d[0], NZ - d[0]) + min(d[1], NX - d[1])))

    def others(axis):
        if axis == "seq":
            return [lax.rem(ms + a, NS) for a in seq_steps]
        return [lax.rem(vz + a, NZ) * NX + lax.rem(vx + c, NX) for a, c in vocab_steps]

    def spread(src, dst, axis):
        me, n = (ms, NS) if axis == "seq" else (mv, NV)
        sems = sem()
        for to in others(axis):
            push(src, dst.at[me], axis, to, sems)
        rest = dst.at[pl.ds(0, n - 1)]
        drains.append((rest, sems[0]))
        return lambda: wait_bytes(rest, sems[1])

    def scatter(src, dst, axis):
        n = NS if axis == "seq" else NV
        sems = sem()
        for i, to in enumerate(others(axis)):
            push(src.at[to], dst.at[i], axis, to, sems)
        rest = dst.at[pl.ds(0, n - 1)]
        drains.append((rest, sems[0]))
        return lambda: wait_bytes(rest, sems[1])

    def one(src, dst, axis, to):
        copy = push(src, dst, axis, to, sem())
        drains.append(copy)
        return copy.wait_recv

    barrier = pltpu.get_barrier_semaphore()
    for step in range(1, NS):
        pl.semaphore_signal(barrier, inc=1, device_id={"seq": lax.rem(ms + step, NS)}, device_id_type=MESH)
    for step in range(1, NV):
        pl.semaphore_signal(barrier, inc=1, device_id={"vocab": lax.rem(mv + step, NV)}, device_id_type=MESH)
    for to in (mate, zmate):
        pl.semaphore_signal(barrier, inc=1, device_id={"dp": to}, device_id_type=MESH)
    w = b.w
    k, v, wo, res, gain, tgt = b.k, b.v, b.wo, b.res, b.gain, b.tgt
    loads = []
    for i, (src, dst) in enumerate(
        ((q_hbm, b.q_all.at[ms]), (k_hbm, k), (v_hbm, v), (wo_hbm, wo), (res_hbm, res), (gain_hbm, gain),
         (tgt_hbm, tgt), (w_hbm, w.at[pl.ds(0, V)]))
    ):
        loads.append(pltpu.make_async_copy(src, dst, b.lsem.at[i]))
        loads[-1].start()
    pl.semaphore_wait(barrier, NS - 1 + NV - 1 + 2)

    got_q = spread(q_hbm, b.q_all, "seq")
    for load in loads[:3]:
        load.wait()
    got_q()
    q_rows = b.q_all[...].reshape(R, HD)
    s = dot(q_rows, k[...], 1, 1) * scale
    place = lax.broadcasted_iota(jnp.int32, (R, KJ), 1) + ms * KJ
    s = jnp.where(place < ln[0], s, -jnp.inf)
    b.s[...] = s
    peak = jnp.maximum(jnp.max(s, axis=1, keepdims=True), -1e30)
    e = jnp.exp(s - peak)
    total = jnp.sum(e, axis=1, keepdims=True)
    denom = jnp.maximum(total, 1e-30)
    e_top = e.astype(BF16)
    e_rest = e - e_top.astype(F32)
    e_mid = e_rest.astype(BF16)
    e_low = (e_rest - e_mid.astype(F32)).astype(BF16)
    acc = dot(e_top, v[...], 1, 0)
    b.acc_send[...] = (acc / denom).astype(BF16).reshape(NS, TR, HD)
    for i in range(NS):
        rows = slice(i * TR, (i + 1) * TR)
        b.st_send[i] = sub_pick([to_row(peak[rows], TR), to_row(total[rows], TR)])
    got_st = scatter(b.st_send, b.st_recv, "seq")
    got_acc = scatter(b.acc_send, b.acc_recv, "seq")
    acc = acc + (dot(e_mid, v[...], 1, 0) + dot(e_low, v[...], 1, 0))
    b.full_send[...] = (acc / denom).reshape(NS, TR, HD)
    for load in loads[3:]:
        load.wait()
    if V < VP:
        w[V:VP] = jnp.zeros((VP - V, C), BF16)
    got_st()
    b.st_recv[NS - 1] = b.st_send[ms]
    tiles = b.st_recv[...]
    top = jnp.max(tiles[:, 0:1], axis=0)
    parts = tiles[:, 1:2] * jnp.exp(tiles[:, 0:1] - top[None])
    whole = jnp.sum(parts, axis=0)
    shares = [to_col(parts[i] / whole, TR) for i in range(NS)]
    b.stat_all[ms] = sub_pick([top, whole])
    got_acc()
    att = b.acc_send[ms].astype(F32) * shares[NS - 1]
    for i in range(NS - 1):
        att = att + b.acc_recv[i].astype(F32) * shares[i]
    b.att_all[ms] = att.astype(BF16)
    got_att = spread(b.att_all.at[ms], b.att_all, "seq")
    got_stat = spread(b.stat_all.at[ms], b.stat_all, "seq")
    got_full = scatter(b.full_send, b.full_recv, "seq")
    got_att()

    mixed_part = dot(b.att_all[...].reshape(R, HD), wo[...], 1, 0)
    b.mix_send[...] = mixed_part.astype(BF16).reshape(NV, RB, C)
    got_mix = scatter(b.mix_send, b.mix_recv, "vocab")
    mine = res[pl.ds(pl.multiple_of(mv * RB, RB), RB), :].astype(F32)
    got_mix()
    mixed = mine + b.mix_send[mv].astype(F32)
    for i in range(NV - 1):
        mixed = mixed + b.mix_recv[i].astype(F32)
    b.mixed[...] = mixed
    b.mg[mv] = (mixed * gain[...]).astype(BF16)
    got_mg = spread(b.mg.at[mv], b.mg, "vocab")
    b.sq[ms] = sub_pick([to_row(jnp.sum(mixed * mixed, axis=1, keepdims=True), RB)])
    got_sq = spread(b.sq.at[ms], b.sq, "seq")
    got_sq()
    square = jnp.sum(b.sq[...], axis=0)[0:1]
    b.inv[mv] = sub_pick([lax.rsqrt(square / D + EPS)])
    got_inv = spread(b.inv.at[mv], b.inv, "vocab")
    got_mg()

    def rows_of(owner):
        return b.mg[pl.ds(owner * NB, NB)].reshape(TR, C)

    def at(distance):
        return lax.rem(ms + distance + NS, NS)

    half = [slice(0, VH), slice(VH, VP)]
    cw_send, cw_recv, cc_send, cc_recv = b.cw_send, b.cw_recv, b.cc_send, b.cc_recv
    cw_got, cc_got = {}, {}
    far = rows_of(at(H))
    for hh in range(2):
        block = dot(far, w[half[hh]], 1, 1)
        if hh == 0:
            cw_send[0, 0] = block
            cw_got[0, 0] = one(cw_send.at[0, 0], cw_recv.at[0, 0], "seq", right)
        else:
            cc_send[0, 1] = block
            cc_got[0, 1] = one(cc_send.at[0, 1], cc_recv.at[0, 1], "seq", left)
    for step in range(1, H):
        both = jnp.concatenate([rows_of(at(H - step)), rows_of(at(step - H))], axis=0)
        for hh in range(2):
            block = dot(both, w[half[hh]], 1, 1)
            cw_send[step, hh] = block[:TR]
            cc_send[step, hh] = block[TR:]
        for hh in range(2):
            for way in ((0, 1) if hh == 0 else (1, 0)):
                sends, recvs, got, to = ((cw_send, cw_recv, cw_got, right), (cc_send, cc_recv, cc_got, left))[way]
                if (step - 1, hh) in got:
                    got[step - 1, hh]()
                    sends[step, hh] = sends[step, hh] + recvs[step - 1, hh]
                got[step, hh] = one(sends.at[step, hh], recvs.at[step, hh], "seq", to)
    own = rows_of(ms)
    for hh in range(2):
        b.logits[:, half[hh]] = dot(own, w[half[hh]], 1, 1)
    got_full()
    att_full = b.full_send[ms] * shares[NS - 1]
    for i in range(NS - 1):
        att_full = att_full + b.full_recv[i] * shares[i]
    b.att_full[...] = att_full
    got_inv()
    normed = []
    for i in range(NV):
        normed.append(b.mg[i].astype(F32) * to_col(b.inv[i][0:1], RB))
    b.normed[...] = jnp.concatenate(normed, axis=0).astype(BF16)
    inv_own = jnp.concatenate([to_col(b.inv[ms * NB + i][0:1], RB) for i in range(NB)], axis=0)
    for hh in range(2):
        block = b.logits[:, half[hh]]
        for got, recvs in ((cw_got, cw_recv), (cc_got, cc_recv)):
            if (H - 1, hh) in got:
                got[H - 1, hh]()
                block = block + recvs[H - 1, hh]
        block = block * inv_own
        if hh == 1:
            col = lax.broadcasted_iota(jnp.int32, (TR, VH), 1) + VH
            block = jnp.where(col < V, block, -jnp.inf)
        b.logits[:, half[hh]] = block

    logits = b.logits[...]
    tgt_col = to_col(jnp.concatenate([tgt[...].astype(F32), jnp.zeros((1, 128 - TR), F32)], axis=1), TR)
    tgt_col = tgt_col.astype(jnp.int32) - mv * V
    col = lax.broadcasted_iota(jnp.int32, (TR, VP), 1)
    hit = jnp.logical_and(col == tgt_col, col < V)
    row_peak = jnp.max(logits, axis=1, keepdims=True)
    row_sum = jnp.sum(jnp.exp(logits - row_peak), axis=1, keepdims=True)
    row_tgt = jnp.sum(jnp.where(hit, logits, 0.0), axis=1, keepdims=True)
    b.stats[mv] = sub_pick([to_row(x, TR) for x in (row_peak, row_sum, row_tgt)])
    got_stats = spread(b.stats.at[mv], b.stats, "vocab")
    got_stats()
    st = b.stats[...]
    tops = jnp.max(st[:, 0:1, :], axis=0)
    sums = jnp.sum(st[:, 1:2, :] * jnp.exp(st[:, 0:1, :] - tops[None]), axis=0)
    hits = jnp.sum(st[:, 2:3, :], axis=0)
    log_total = tops + jnp.log(sums)
    loss = log_total - hits + ZW * log_total * log_total
    lane = lax.broadcasted_iota(jnp.int32, (1, 128), 1)
    loss = jnp.where(lane < TR, loss, 0.0)
    lt = to_col(jnp.where(lane < TR, log_total, 0.0), TR)
    grad = jnp.exp(logits - lt) * (1.0 + 2.0 * ZW * lt) - hit.astype(F32)
    grad = grad.astype(BF16)
    g_all = b.g_all
    VQ = VP // 4
    along = jnp.sum(jnp.where(col < V, grad.astype(F32) * logits, 0.0), axis=1, keepdims=True)
    b.along[mv] = sub_pick([to_row(along, TR)])
    for i in range(4):
        g_all[ms, i] = grad[:, i * VQ:(i + 1) * VQ]

    cw_got, cc_got = {}, {}

    def forward(step, hh, way):
        if step == H - 1 and hh != way:
            return
        got, to, owner = ((cw_got, right, at(-step)), (cc_got, left, at(step)))[way]
        if step > 0:
            got[step - 1, hh]()
        piece = g_all.at[owner, pl.ds(2 * hh, 2)]
        got[step, hh] = one(piece, piece, "seq", to)

    hid_sems = sem()
    b_hid = b.hid_recv

    def hidden(owners):
        out = None
        for i in range(4):
            rows = jnp.concatenate([g_all[o, i] for o in owners], axis=0)
            term = dot(rows, w[i * VQ:(i + 1) * VQ], 1, 0)
            out = term if out is None else out + term
        out = out.astype(BF16)
        for i, o in enumerate(owners):
            b.hid_send[pl.ds(o * NB, NB)] = out[i * TR:(i + 1) * TR].reshape(NB, RB, C)
            for part in range(NB):
                to = o * NB + part

                @pl.when(to != mv)
                def _():
                    push(b.hid_send.at[to], b_hid.at[mv], "vocab", to, hid_sems)

    for step in range(H):
        for hh in range(2):
            for way in range(2):
                forward(step, hh, way)
        if step == 0:
            got_along = spread(b.along.at[mv], b.along, "vocab")
            hidden([ms])
        else:
            for got in (cw_got, cc_got):
                for hh in range(2):
                    if step == H - 1 and (step, hh) not in got:
                        got[step - 1, hh]()
            hidden([at(-step), at(step)])
        if step == min(1, H - 1):
            got_along()
            b.loss[ms] = sub_pick([loss, jnp.sum(b.along[...], axis=0)[0:1]])
            got_loss = spread(b.loss.at[ms], b.loss, "seq")
    cw_got[H - 1, 0]()
    cc_got[H - 1, 1]()
    hidden([at(H)])

    def head(quarter):
        return dot(g_all[:, quarter].reshape(R, VQ), b.normed[...], 0, 0).astype(BF16)

    got_half = []
    for i in range(2):
        b.hg_send[i] = head(2 * (1 - core) + i)
        got_half.append(one(b.hg_send.at[i], b.hg_recv.at[i], "dp", mate))
    for i in range(2):
        b.hg_own[i] = head(2 * core + i)
    got_pair = []
    for i in range(2):
        got_half[i]()
        b.hg_pair[i] = (b.hg_own[i].astype(F32) + b.hg_recv[i].astype(F32)).astype(BF16)
        got_pair.append(one(b.hg_pair.at[i], b.hg_far.at[i], "dp", zmate))

    rest = b_hid.at[pl.ds(0, NV - 1)]
    drains.append((rest, hid_sems[0]))
    wait_bytes(rest, hid_sems[1])
    b_hid[mv] = b.hid_send[mv]
    gated = jnp.sum(b_hid[...].astype(F32), axis=0) * gain[...]
    got_loss()
    b.loss1[0] = jnp.sum(b.loss[...], axis=0)
    got_l1 = one(b.loss1.at[0], b.loss1.at[1], "dp", mate)
    row = lax.broadcasted_iota(jnp.int32, (RB, 128), 0) + lax.rem(mv, NB) * RB
    lane = lax.broadcasted_iota(jnp.int32, (RB, 128), 1)
    tile = jnp.broadcast_to(b.loss[mv // NB][1:2], (RB, 128))
    along = jnp.sum(jnp.where(row == lane, tile, 0.0), axis=1, keepdims=True)
    inv = to_col(b.inv[mv][0:1], RB)
    mixed_grad = gated * inv - b.mixed[...] * (inv * inv * along / D)
    b.mgrad[mv] = mixed_grad.astype(BF16)
    got_mgrad = spread(b.mgrad.at[mv], b.mgrad, "vocab")
    got_l1()
    b.loss2[0] = b.loss1[0] + b.loss1[1]
    got_l2 = one(b.loss2.at[0], b.loss2.at[1], "dp", zmate)
    got_stat()
    tops = jnp.concatenate([to_col(b.stat_all[i][0:1], TR) for i in range(NS)], axis=0)
    sums = jnp.concatenate([to_col(b.stat_all[i][1:2], TR) for i in range(NS)], axis=0)
    weights = jnp.exp(b.s[...] - tops) / sums
    b.s[...] = weights

    got_mgrad()
    ag_part = dot(b.mgrad[...].reshape(R, C), wo[...], 1, 1)
    b.ag_send[...] = ag_part.astype(BF16).reshape(NS, TR, HD)
    got_ag = scatter(b.ag_send, b.ag_recv, "seq")
    got_ag()
    ag = b.ag_send[ms].astype(F32)
    for i in range(NS - 1):
        ag = ag + b.ag_recv[i].astype(F32)
    ag = ag.astype(BF16)
    b.ag_all[ms] = ag
    got_ag_all = spread(b.ag_all.at[ms], b.ag_all, "seq")
    delta = jnp.sum(ag.astype(F32) * b.att_full[...], axis=1, keepdims=True)
    b.delta[ms] = sub_pick([to_row(delta, TR)])
    got_delta = spread(b.delta.at[ms], b.delta, "seq")
    fin = b.fin

    def finish_half(i):
        got_pair[i]()
        fin[2 * core + i] = (b.hg_pair[i].astype(F32) + b.hg_far[i].astype(F32)).astype(BF16)
        piece = fin.at[2 * core + i]
        return one(piece, piece, "dp", mate)

    got_fin = [finish_half(0)]
    got_ag_all()
    got_delta()
    ag_rows = b.ag_all[...].reshape(R, HD)
    prob_grad = dot(ag_rows, v[...], 1, 1)
    delta = jnp.concatenate([to_col(b.delta[i][0:1], TR) for i in range(NS)], axis=0)
    weights = b.s[...]
    score_grad = (weights * (prob_grad - delta) * scale).astype(BF16)
    b.kg[...] = dot(score_grad, b.q_all[...].reshape(R, HD), 0, 0)
    b.vg[...] = dot(weights.astype(BF16), ag_rows, 0, 0)
    stores = []
    for i, (src, dst) in enumerate(((b.kg, out_kg), (b.vg, out_vg))):
        stores.append(pltpu.make_async_copy(src, dst, b.lsem.at[12 + i]))
        stores[-1].start()
    got_l2()
    loss = (b.loss2[0] + b.loss2[1])[0:1]
    out_loss[...] = jnp.sum(loss, axis=1, keepdims=True) / batch_rows
    got_fin.append(finish_half(1))
    for got in got_fin:
        got()
    for i in range(4):
        size = min(VQ, V - i * VQ)
        if size > 0:
            store = pltpu.make_async_copy(fin.at[i, pl.ds(0, size)], out_hg.at[pl.ds(i * VQ, size)], b.lsem.at[8 + i])
            store.start()
            stores.append(store)
    for item in drains:
        if isinstance(item, tuple):
            wait_bytes(*item)
        else:
            item.wait_send()
    for store in stores:
        store.wait()


def scratch_list(cfg):
    NS, NV, TR, KJ, C, V, VP, batch_rows = cfg
    HD = HDIM
    R = TR * NS
    RB = R // NV
    H = NS // 2
    VH = VP // 2

    def vm(*shape, dtype=BF16):
        return pltpu.VMEM(shape, dtype)

    return dict(
        gain=vm(1, C, dtype=F32), tgt=vm(1, TR, dtype=jnp.int32),
        k=vm(KJ, HD), v=vm(KJ, HD), wo=vm(HD, C), res=vm(R, C), w=vm(VP, C),
        q_all=vm(NS, TR, HD), s=vm(R, KJ, dtype=F32),
        acc_send=vm(NS, TR, HD), acc_recv=vm(NS, TR, HD),
        st_send=vm(NS, 8, 128, dtype=F32), st_recv=vm(NS, 8, 128, dtype=F32),
        full_send=vm(NS, TR, HD, dtype=F32), full_recv=vm(NS, TR, HD, dtype=F32), att_full=vm(TR, HD, dtype=F32),
        att_all=vm(NS, TR, HD), stat_all=vm(NS, 8, 128, dtype=F32),
        mix_send=vm(NV, RB, C), mix_recv=vm(NV, RB, C), mixed=vm(RB, C, dtype=F32),
        mg=vm(NV, RB, C), sq=vm(NS, 8, 128, dtype=F32), inv=vm(NV, 8, 128, dtype=F32),
        cw_send=vm(H, 2, TR, VH, dtype=F32), cw_recv=vm(H, 2, TR, VH, dtype=F32),
        cc_send=vm(H, 2, TR, VH, dtype=F32), cc_recv=vm(H, 2, TR, VH, dtype=F32),
        logits=vm(TR, VP, dtype=F32), stats=vm(NV, 8, 128, dtype=F32),
        normed=vm(R, C), g_all=vm(NS, 4, TR, VP // 4),
        loss=vm(NS, 8, 128, dtype=F32), loss1=vm(2, 8, 128, dtype=F32),
        loss2=vm(2, 8, 128, dtype=F32),
        hid_send=vm(NV, RB, C), hid_recv=vm(NV, RB, C), along=vm(NV, 8, 128, dtype=F32),
        mgrad=vm(NV, RB, C), ag_send=vm(NS, TR, HD), ag_recv=vm(NS, TR, HD),
        ag_all=vm(NS, TR, HD), delta=vm(NS, 8, 128, dtype=F32),
        hg_send=vm(2, VP // 4, C), hg_recv=vm(2, VP // 4, C), hg_own=vm(2, VP // 4, C),
        hg_pair=vm(2, VP // 4, C), hg_far=vm(2, VP // 4, C), fin=vm(4, VP // 4, C),
        kg=vm(KJ, HD, dtype=F32), vg=vm(KJ, HD, dtype=F32),
        ssem=pltpu.SemaphoreType.DMA((80,)), rsem=pltpu.SemaphoreType.DMA((80,)),
        lsem=pltpu.SemaphoreType.DMA((14,)),
    )


def body(sizes, queries, enc_keys, enc_values, enc_lengths, out_proj, residual, norm_gain, head_weight, targets):
    ND, NS, NV = sizes
    TR = queries.shape[1]
    KJ = enc_keys.shape[1]
    C, V = head_weight.shape
    VP = (V + 511) // 512 * 512
    cfg = (NS, NV, TR, KJ, C, V, VP, ND * TR * NS)
    vmem = pl.BlockSpec(memory_space=pltpu.VMEM)
    hbm = pl.BlockSpec(memory_space=pltpu.HBM)
    call = pl.pallas_call(
        functools.partial(kernel, cfg),
        out_shape=(
            jax.ShapeDtypeStruct((1, 1), F32),
            jax.ShapeDtypeStruct((V, C), BF16),
            jax.ShapeDtypeStruct((KJ, HDIM), F32),
            jax.ShapeDtypeStruct((KJ, HDIM), F32),
        ),
        in_specs=[hbm, hbm, hbm, pl.BlockSpec(memory_space=pltpu.SMEM), hbm, hbm, hbm, hbm, hbm],
        out_specs=(vmem, hbm, hbm, hbm),
        scratch_shapes=list(scratch_list(cfg).values()),
        compiler_params=pltpu.CompilerParams(
            collective_id=0, has_side_effects=True, vmem_limit_bytes=63 * 1024 * 1024),
    )
    loss, hg, kg, vg = call(
        queries[0], enc_keys[0], enc_values[0], enc_lengths, out_proj, residual[0],
        norm_gain.reshape(1, C), head_weight.T, targets)
    return (loss.reshape(()), hg.T, kg[None], vg[None])


def solution(mesh):
    placed = (
        P("dp", "seq", "vocab"),
        P("dp", "seq", "vocab"),
        P("dp", "seq", "vocab"),
        P("dp"),
        P("vocab", "seq"),
        P("dp", None, "seq"),
        P("seq"),
        P("seq", "vocab"),
        P("dp", "seq"),
    )
    sizes = (mesh.shape["dp"], mesh.shape["seq"], mesh.shape["vocab"])
    return jax.shard_map(
        functools.partial(body, sizes),
        mesh=mesh,
        in_specs=placed,
        out_specs=(P(), P("seq", "vocab"), P("dp", "seq", "vocab"), P("dp", "seq", "vocab")),
        check_vma=False,
    )
```

time: 161 us -> 154 us (0.957)
  local copies, waits for them, and re-layouts: 9.5 us -> 4.37 us
    unnamed x20 -> x7, local copies, waits for them, and re-layouts: 9.5 us -> 4.37 us
where the time goes in v2:
time: 154 us
  Pallas kernels  147 us (95%)
  local copies, waits for them, and re-layouts  4.37 us (3%)
  between operations  3.06 us (2%)
    pallas_call x1, Pallas kernels, body(): call(queries[0], enc_keys[0], enc_values[0], enc_lengths, out_proj, resid...  147 us
    unnamed x7, local copies, waits for them, and re-layouts  4.37 us

profile of v2, /device:TPU:1, one launch (start us, length us, event | category | flops | bytes accessed | tf_op | source)
XLA Modules:
  0.0 154.2 jit_solution(15213690357366543828)
XLA Ops:
  1.3 146.8 %shard_map.120 = (f32[1,1]{1,0:T(1,128)}, bf16[2008,512]{1,0:T(8,128)(2,1)}, f32[128,256]{1,0:T(8,128)}, f32[128,256]{1,0:T(8,128)}) custom-call(bf16[32,256]{1,0:T(8,128)(2,1)} %bitcast.17, bf16[128,256]{1,0:T(8,128)(2,1)} %bitcast.15, bf16[128,256]{1,0:T(8,128)(2,1)} %bitcast.16, s32[1]{0:T(128)S(6)} %copy.17.ln, bf16[256,512]{1,0:T(8,128)(2,1)} %wo_hbm.1, ...), custom_call_target="tpu_custom_call" | custom-call | tf_op jit(solution)/shard_map/pallas_call | solution.py:495
  148.7 0.0 copy-start.1
  148.7 0.0 copy-start
  148.7 3.1 %copy.19 = bf16[512,2008]{0,1:T(8,128)(2,1)} copy(bf16[512,2008]{0,1:T(8,128)(2,1)} %bitcast.11) | data formatting | bytes 4112384
  151.7 0.0 copy-done.1
  151.7 0.7 copy.20
  152.4 0.0 copy-done
  152.4 0.7 copy.21
Async XLA Ops:
  148.7 3.1 %copy-start.1 = (f32[128,256]{1,0:T(8,128)S(1)}, f32[128,256]{1,0:T(8,128)}, u32[]{:S(2)}) copy-start(f32[128,256]{1,0:T(8,128)} %get-tuple-element.10) | copy-start | bytes 393220
  148.7 3.7 %copy-start = (f32[128,256]{1,0:T(8,128)S(1)}, f32[128,256]{1,0:T(8,128)}, u32[]{:S(2)}) copy-start(f32[128,256]{1,0:T(8,128)} %get-tuple-element.11) | copy-start | bytes 393220

commit v3 on v2

--- a/solution.py
+++ b/solution.py
@@ -240,7 +240,8 @@
     normed = []
     for i in range(NV):
         normed.append(b.mg[i].astype(F32) * to_col(b.inv[i][0:1], RB))
-    b.normed[...] = jnp.concatenate(normed, axis=0).astype(BF16)
+    b.normed[zlo] = jnp.concatenate(normed, axis=0).astype(BF16)
+    got_normed = one(b.normed.at[zlo], b.normed.at[zlo], "dp", zmate)
     inv_own = jnp.concatenate([to_col(b.inv[ms * NB + i][0:1], RB) for i in range(NB)], axis=0)
     for hh in range(2):
         block = b.logits[:, half[hh]]
@@ -276,24 +277,38 @@
     lt = to_col(jnp.where(lane < TR, log_total, 0.0), TR)
     grad = jnp.exp(logits - lt) * (1.0 + 2.0 * ZW * lt) - hit.astype(F32)
     grad = grad.astype(BF16)
-    g_all = b.g_all
+    g_all = b.g_all.at[zlo]
+    g_far = b.g_all.at[1 - zlo]
     VQ = VP // 4
     along = jnp.sum(jnp.where(col < V, grad.astype(F32) * logits, 0.0), axis=1, keepdims=True)
     b.along[mv] = sub_pick([to_row(along, TR)])
     for i in range(4):
         g_all[ms, i] = grad[:, i * VQ:(i + 1) * VQ]
 
-    cw_got, cc_got = {}, {}
-
-    def forward(step, hh, way):
-        if step == H - 1 and hh != way:
-            return
-        got, to, owner = ((cw_got, right, at(-step)), (cc_got, left, at(step)))[way]
-        if step > 0:
-            got[step - 1, hh]()
-        piece = g_all.at[owner, pl.ds(2 * hh, 2)]
-        got[step, hh] = one(piece, piece, "seq", to)
-
+    got_z = one(g_all.at[ms], g_all.at[ms], "dp", zmate)
+
+    def ring(buf):
+        cw_got, cc_got = {}, {}
+
+        def forward(step):
+            for hh in range(2):
+                for way in range(2):
+                    got, to, owner = ((cw_got, right, at(-step)), (cc_got, left, at(step)))[way]
+                    if step > 0:
+                        got[step - 1, hh]()
+                    if step == H - 1 and hh != way:
+                        continue
+                    piece = buf.at[owner, pl.ds(2 * hh, 2)]
+                    got[step, hh] = one(piece, piece, "seq", to)
+
+        def last():
+            cw_got[H - 1, 0]()
+            cc_got[H - 1, 1]()
+
+        return forward, last
+
+    forward, last = ring(g_all)
+    far_forward, far_last = ring(g_far)
     hid_sems = sem()
     b_hid = b.hid_recv
 
@@ -314,40 +329,22 @@
                     push(b.hid_send.at[to], b_hid.at[mv], "vocab", to, hid_sems)
 
     for step in range(H):
-        for hh in range(2):
-            for way in range(2):
-                forward(step, hh, way)
+        forward(step)
         if step == 0:
             got_along = spread(b.along.at[mv], b.along, "vocab")
             hidden([ms])
         else:
-            for got in (cw_got, cc_got):
-                for hh in range(2):
-                    if step == H - 1 and (step, hh) not in got:
-                        got[step - 1, hh]()
             hidden([at(-step), at(step)])
         if step == min(1, H - 1):
             got_along()
             b.loss[ms] = sub_pick([loss, jnp.sum(b.along[...], axis=0)[0:1]])
             got_loss = spread(b.loss.at[ms], b.loss, "seq")
-    cw_got[H - 1, 0]()
-    cc_got[H - 1, 1]()
+    got_z()
+    far_forward(0)
+    last()
     hidden([at(H)])
-
-    def head(quarter):
-        return dot(g_all[:, quarter].reshape(R, VQ), b.normed[...], 0, 0).astype(BF16)
-
-    got_half = []
-    for i in range(2):
-        b.hg_send[i] = head(2 * (1 - core) + i)
-        got_half.append(one(b.hg_send.at[i], b.hg_recv.at[i], "dp", mate))
-    for i in range(2):
-        b.hg_own[i] = head(2 * core + i)
-    got_pair = []
-    for i in range(2):
-        got_half[i]()
-        b.hg_pair[i] = (b.hg_own[i].astype(F32) + b.hg_recv[i].astype(F32)).astype(BF16)
-        got_pair.append(one(b.hg_pair.at[i], b.hg_far.at[i], "dp", zmate))
+    for step in range(1, min(2, H)):
+        far_forward(step)
 
     rest = b_hid.at[pl.ds(0, NV - 1)]
     drains.append((rest, hid_sems[0]))
@@ -365,6 +362,8 @@
     mixed_grad = gated * inv - b.mixed[...] * (inv * inv * along / D)
     b.mgrad[mv] = mixed_grad.astype(BF16)
     got_mgrad = spread(b.mgrad.at[mv], b.mgrad, "vocab")
+    for step in range(2, H):
+        far_forward(step)
     got_l1()
     b.loss2[0] = b.loss1[0] + b.loss1[1]
     got_l2 = one(b.loss2.at[0], b.loss2.at[1], "dp", zmate)
@@ -378,6 +377,16 @@
     ag_part = dot(b.mgrad[...].reshape(R, C), wo[...], 1, 1)
     b.ag_send[...] = ag_part.astype(BF16).reshape(NS, TR, HD)
     got_ag = scatter(b.ag_send, b.ag_recv, "seq")
+
+    def head(quarter):
+        return dot(b.g_all[:, :, quarter].reshape(2 * R, VQ), b.normed[...].reshape(2 * R, C), 0, 0).astype(BF16)
+
+    far_last()
+    got_normed()
+    got_half = []
+    for i in range(2):
+        b.hg_send[i] = head(2 * (1 - core) + i)
+        got_half.append(one(b.hg_send.at[i], b.hg_recv.at[i], "dp", mate))
     got_ag()
     ag = b.ag_send[ms].astype(F32)
     for i in range(NS - 1):
@@ -389,14 +398,13 @@
     b.delta[ms] = sub_pick([to_row(delta, TR)])
     got_delta = spread(b.delta.at[ms], b.delta, "seq")
     fin = b.fin
-
-    def finish_half(i):
-        got_pair[i]()
-        fin[2 * core + i] = (b.hg_pair[i].astype(F32) + b.hg_far[i].astype(F32)).astype(BF16)
+    got_fin = []
+    for i in range(2):
+        b.hg_own[i] = head(2 * core + i)
+        got_half[i]()
         piece = fin.at[2 * core + i]
-        return one(piece, piece, "dp", mate)
-
-    got_fin = [finish_half(0)]
+        piece[...] = (b.hg_own[i].astype(F32) + b.hg_recv[i].astype(F32)).astype(BF16)
+        got_fin.append(one(piece, piece, "dp", mate))
     got_ag_all()
     got_delta()
     ag_rows = b.ag_all[...].reshape(R, HD)
@@ -413,7 +421,6 @@
     got_l2()
     loss = (b.loss2[0] + b.loss2[1])[0:1]
     out_loss[...] = jnp.sum(loss, axis=1, keepdims=True) / batch_rows
-    got_fin.append(finish_half(1))
     for got in got_fin:
         got()
     for i in range(4):
@@ -455,14 +462,14 @@
         cw_send=vm(H, 2, TR, VH, dtype=F32), cw_recv=vm(H, 2, TR, VH, dtype=F32),
         cc_send=vm(H, 2, TR, VH, dtype=F32), cc_recv=vm(H, 2, TR, VH, dtype=F32),
         logits=vm(TR, VP, dtype=F32), stats=vm(NV, 8, 128, dtype=F32),
-        normed=vm(R, C), g_all=vm(NS, 4, TR, VP // 4),
+        normed=vm(2, R, C), g_all=vm(2, NS, 4, TR, VP // 4),
         loss=vm(NS, 8, 128, dtype=F32), loss1=vm(2, 8, 128, dtype=F32),
         loss2=vm(2, 8, 128, dtype=F32),
         hid_send=vm(NV, RB, C), hid_recv=vm(NV, RB, C), along=vm(NV, 8, 128, dtype=F32),
         mgrad=vm(NV, RB, C), ag_send=vm(NS, TR, HD), ag_recv=vm(NS, TR, HD),
         ag_all=vm(NS, TR, HD), delta=vm(NS, 8, 128, dtype=F32),
         hg_send=vm(2, VP // 4, C), hg_recv=vm(2, VP // 4, C), hg_own=vm(2, VP // 4, C),
-        hg_pair=vm(2, VP // 4, C), hg_far=vm(2, VP // 4, C), fin=vm(4, VP // 4, C),
+        fin=vm(4, VP // 4, C),
         kg=vm(KJ, HD, dtype=F32), vg=vm(KJ, HD, dtype=F32),
         ssem=pltpu.SemaphoreType.DMA((80,)), rsem=pltpu.SemaphoreType.DMA((80,)),
         lsem=pltpu.SemaphoreType.DMA((14,)),

time: 154 us -> 133 us (0.86); the launches traced: 154 us -> 131 us
  Pallas kernels: 147 us -> 123 us
    pallas_call x1, Pallas kernels: 147 us -> 123 us  [body(): call(queries[0], enc_keys[0], enc_values[0], enc_lengths, out_proj, resid...]
where the time goes in v3:
time: 133 us; the launch traced here: 131 us
  Pallas kernels  123 us (92%)
  local copies, waits for them, and re-layouts  4.37 us (3%)
  between operations  3.06 us (2%)
    pallas_call x1, Pallas kernels, body(): call(queries[0], enc_keys[0], enc_values[0], enc_lengths, out_proj, resid...  123 us
    unnamed x7, local copies, waits for them, and re-layouts  4.37 us

profile of v3, /device:TPU:1, one launch (start us, length us, event | category | flops | bytes accessed | tf_op | source)
XLA Modules:
  0.0 130.5 jit_solution(15885543979078263134)
XLA Ops:
  1.3 123.1 %shard_map.120 = (f32[1,1]{1,0:T(1,128)}, bf16[2008,512]{1,0:T(8,128)(2,1)}, f32[128,256]{1,0:T(8,128)}, f32[128,256]{1,0:T(8,128)}) custom-call(bf16[32,256]{1,0:T(8,128)(2,1)} %bitcast.17, bf16[128,256]{1,0:T(8,128)(2,1)} %bitcast.15, bf16[128,256]{1,0:T(8,128)(2,1)} %bitcast.16, s32[1]{0:T(128)S(6)} %copy.17.ln, bf16[256,512]{1,0:T(8,128)(2,1)} %wo_hbm.1, ...), custom_call_target="tpu_custom_call" | custom-call | tf_op jit(solution)/shard_map/pallas_call | solution.py:502
  125.0 0.0 copy-start.1
  125.0 0.0 copy-start
  125.0 3.1 %copy.19 = bf16[512,2008]{0,1:T(8,128)(2,1)} copy(bf16[512,2008]{0,1:T(8,128)(2,1)} %bitcast.11) | data formatting | bytes 4112384
  128.1 0.0 copy-done.1
  128.1 0.7 copy.20
  128.7 0.0 copy-done
  128.7 0.7 copy.21
Async XLA Ops:
  125.0 3.1 %copy-start.1 = (f32[128,256]{1,0:T(8,128)S(1)}, f32[128,256]{1,0:T(8,128)}, u32[]{:S(2)}) copy-start(f32[128,256]{1,0:T(8,128)} %get-tuple-element.10) | copy-start | bytes 393220
  125.0 3.7 %copy-start = (f32[128,256]{1,0:T(8,128)S(1)}, f32[128,256]{1,0:T(8,128)}, u32[]{:S(2)}) copy-start(f32[128,256]{1,0:T(8,128)} %get-tuple-element.11) | copy-start | bytes 393220

commit v4 on v3

--- a/solution.py
+++ b/solution.py
@@ -13,6 +13,7 @@
 EPS = 1e-06
 MESH = pl.DeviceIdType.MESH
 F32 = jnp.float32
+SEMS = 128
 BF16 = jnp.bfloat16
 
 
@@ -48,7 +49,6 @@
     RB = R // NV
     NB = TR // RB
     H = NS // 2
-    VH = VP // 2
     D = C * NS
     scale = HD ** (-0.5)
     md, ms, mv = lax.axis_index("dp"), lax.axis_index("seq"), lax.axis_index("vocab")
@@ -203,34 +203,32 @@
     def at(distance):
         return lax.rem(ms + distance + NS, NS)
 
-    half = [slice(0, VH), slice(VH, VP)]
-    cw_send, cw_recv, cc_send, cc_recv = b.cw_send, b.cw_recv, b.cc_send, b.cc_recv
-    cw_got, cc_got = {}, {}
+    VQ = VP // 4
+    part = [slice(i * VQ, (i + 1) * VQ) for i in range(4)]
+    order = ((0, 1, 2, 3), (2, 3, 0, 1))
+    sends, recvs, gots = (b.cw_send, b.cc_send), (b.cw_recv, b.cc_recv), ({}, {})
+    toward = (right, left)
     far = rows_of(at(H))
-    for hh in range(2):
-        block = dot(far, w[half[hh]], 1, 1)
-        if hh == 0:
-            cw_send[0, 0] = block
-            cw_got[0, 0] = one(cw_send.at[0, 0], cw_recv.at[0, 0], "seq", right)
-        else:
-            cc_send[0, 1] = block
-            cc_got[0, 1] = one(cc_send.at[0, 1], cc_recv.at[0, 1], "seq", left)
+    for i in (0, 2, 1, 3):
+        way = i // 2
+        sends[way][0, i] = dot(far, w[part[i]], 1, 1)
+        gots[way][0, i] = one(sends[way].at[0, i], recvs[way].at[0, i], "seq", toward[way])
     for step in range(1, H):
         both = jnp.concatenate([rows_of(at(H - step)), rows_of(at(step - H))], axis=0)
-        for hh in range(2):
-            block = dot(both, w[half[hh]], 1, 1)
-            cw_send[step, hh] = block[:TR]
-            cc_send[step, hh] = block[TR:]
-        for hh in range(2):
-            for way in ((0, 1) if hh == 0 else (1, 0)):
-                sends, recvs, got, to = ((cw_send, cw_recv, cw_got, right), (cc_send, cc_recv, cc_got, left))[way]
-                if (step - 1, hh) in got:
-                    got[step - 1, hh]()
-                    sends[step, hh] = sends[step, hh] + recvs[step - 1, hh]
-                got[step, hh] = one(sends.at[step, hh], recvs.at[step, hh], "seq", to)
+        for i in range(4):
+            block = dot(both, w[part[i]], 1, 1)
+            sends[0][step, i] = block[:TR]
+            sends[1][step, i] = block[TR:]
+        for n in range(4):
+            for way in range(2):
+                i = order[way][n]
+                if (step - 1, i) in gots[way]:
+                    gots[way][step - 1, i]()
+                    sends[way][step, i] = sends[way][step, i] + recvs[way][step - 1, i]
+                gots[way][step, i] = one(sends[way].at[step, i], recvs[way].at[step, i], "seq", toward[way])
     own = rows_of(ms)
-    for hh in range(2):
-        b.logits[:, half[hh]] = dot(own, w[half[hh]], 1, 1)
+    for i in range(4):
+        b.logits[:, part[i]] = dot(own, w[part[i]], 1, 1)
     got_full()
     att_full = b.full_send[ms] * shares[NS - 1]
     for i in range(NS - 1):
@@ -243,17 +241,17 @@
     b.normed[zlo] = jnp.concatenate(normed, axis=0).astype(BF16)
     got_normed = one(b.normed.at[zlo], b.normed.at[zlo], "dp", zmate)
     inv_own = jnp.concatenate([to_col(b.inv[ms * NB + i][0:1], RB) for i in range(NB)], axis=0)
-    for hh in range(2):
-        block = b.logits[:, half[hh]]
-        for got, recvs in ((cw_got, cw_recv), (cc_got, cc_recv)):
-            if (H - 1, hh) in got:
-                got[H - 1, hh]()
-                block = block + recvs[H - 1, hh]
+    for i in range(4):
+        block = b.logits[:, part[i]]
+        for way in range(2):
+            if (H - 1, i) in gots[way]:
+                gots[way][H - 1, i]()
+                block = block + recvs[way][H - 1, i]
         block = block * inv_own
-        if hh == 1:
-            col = lax.broadcasted_iota(jnp.int32, (TR, VH), 1) + VH
+        if (i + 1) * VQ > V:
+            col = lax.broadcasted_iota(jnp.int32, (TR, VQ), 1) + i * VQ
             block = jnp.where(col < V, block, -jnp.inf)
-        b.logits[:, half[hh]] = block
+        b.logits[:, part[i]] = block
 
     logits = b.logits[...]
     tgt_col = to_col(jnp.concatenate([tgt[...].astype(F32), jnp.zeros((1, 128 - TR), F32)], axis=1), TR)
@@ -279,7 +277,6 @@
     grad = grad.astype(BF16)
     g_all = b.g_all.at[zlo]
     g_far = b.g_all.at[1 - zlo]
-    VQ = VP // 4
     along = jnp.sum(jnp.where(col < V, grad.astype(F32) * logits, 0.0), axis=1, keepdims=True)
     b.along[mv] = sub_pick([to_row(along, TR)])
     for i in range(4):
@@ -291,19 +288,20 @@
         cw_got, cc_got = {}, {}
 
         def forward(step):
-            for hh in range(2):
+            for n in range(4):
                 for way in range(2):
-                    got, to, owner = ((cw_got, right, at(-step)), (cc_got, left, at(step)))[way]
+                    i = order[way][n]
+                    got, owner = ((cw_got, at(-step)), (cc_got, at(step)))[way]
                     if step > 0:
-                        got[step - 1, hh]()
-                    if step == H - 1 and hh != way:
+                        got[step - 1, i]()
+                    if step == H - 1 and i // 2 != way:
                         continue
-                    piece = buf.at[owner, pl.ds(2 * hh, 2)]
-                    got[step, hh] = one(piece, piece, "seq", to)
+                    piece = buf.at[owner, i]
+                    got[step, i] = one(piece, piece, "seq", toward[way])
 
         def last():
-            cw_got[H - 1, 0]()
-            cc_got[H - 1, 1]()
+            for i in range(4):
+                (cw_got, cc_got)[i // 2][H - 1, i]()
 
         return forward, last
 
@@ -444,7 +442,6 @@
     R = TR * NS
     RB = R // NV
     H = NS // 2
-    VH = VP // 2
 
     def vm(*shape, dtype=BF16):
         return pltpu.VMEM(shape, dtype)
@@ -459,8 +456,8 @@
         att_all=vm(NS, TR, HD), stat_all=vm(NS, 8, 128, dtype=F32),
         mix_send=vm(NV, RB, C), mix_recv=vm(NV, RB, C), mixed=vm(RB, C, dtype=F32),
         mg=vm(NV, RB, C), sq=vm(NS, 8, 128, dtype=F32), inv=vm(NV, 8, 128, dtype=F32),
-        cw_send=vm(H, 2, TR, VH, dtype=F32), cw_recv=vm(H, 2, TR, VH, dtype=F32),
-        cc_send=vm(H, 2, TR, VH, dtype=F32), cc_recv=vm(H, 2, TR, VH, dtype=F32),
+        cw_send=vm(H, 4, TR, VP // 4, dtype=F32), cw_recv=vm(H, 4, TR, VP // 4, dtype=F32),
+        cc_send=vm(H, 4, TR, VP // 4, dtype=F32), cc_recv=vm(H, 4, TR, VP // 4, dtype=F32),
         logits=vm(TR, VP, dtype=F32), stats=vm(NV, 8, 128, dtype=F32),
         normed=vm(2, R, C), g_all=vm(2, NS, 4, TR, VP // 4),
         loss=vm(NS, 8, 128, dtype=F32), loss1=vm(2, 8, 128, dtype=F32),
@@ -471,9 +468,24 @@
         hg_send=vm(2, VP // 4, C), hg_recv=vm(2, VP // 4, C), hg_own=vm(2, VP // 4, C),
         fin=vm(4, VP // 4, C),
         kg=vm(KJ, HD, dtype=F32), vg=vm(KJ, HD, dtype=F32),
-        ssem=pltpu.SemaphoreType.DMA((80,)), rsem=pltpu.SemaphoreType.DMA((80,)),
+        ssem=pltpu.SemaphoreType.DMA((SEMS,)), rsem=pltpu.SemaphoreType.DMA((SEMS,)),
         lsem=pltpu.SemaphoreType.DMA((14,)),
     )
+
+
+def tail(hg, kg, vg, hg_out, kg_out, vg_out, hg_mid, kg_mid, vg_mid, sems, sems_out):
+    rows = hg.shape[0] // 64 * 16
+    steps = [(hg, hg_mid, hg_out, pl.ds(i * rows, rows if i < 3 else hg.shape[0] - 3 * rows)) for i in range(4)]
+    steps += [(kg, kg_mid, kg_out, pl.ds(0, kg.shape[0])), (vg, vg_mid, vg_out, pl.ds(0, vg.shape[0]))]
+    loads = [pltpu.make_async_copy(a.at[d], m.at[d], sems.at[i]) for i, (a, m, _, d) in enumerate(steps)]
+    stores = [pltpu.make_async_copy(m.at[d], o.at[d], sems_out.at[i]) for i, (_, m, o, d) in enumerate(steps)]
+    for load in loads:
+        load.start()
+    for load, store in zip(loads, stores):
+        load.wait()
+        store.start()
+    for store in stores:
+        store.wait()
 
 
 def body(sizes, queries, enc_keys, enc_values, enc_lengths, out_proj, residual, norm_gain, head_weight, targets):
@@ -502,6 +514,14 @@
     loss, hg, kg, vg = call(
         queries[0], enc_keys[0], enc_values[0], enc_lengths, out_proj, residual[0],
         norm_gain.reshape(1, C), head_weight.T, targets)
+    hg, kg, vg = pl.pallas_call(
+        tail,
+        out_shape=tuple(jax.ShapeDtypeStruct(x.shape, x.dtype) for x in (hg, kg, vg)),
+        in_specs=[hbm] * 3,
+        out_specs=(hbm,) * 3,
+        scratch_shapes=[pltpu.VMEM(x.shape, x.dtype) for x in (hg, kg, vg)] + [pltpu.SemaphoreType.DMA((6,))] * 2,
+        compiler_params=pltpu.CompilerParams(vmem_limit_bytes=63 * 1024 * 1024),
+    )(hg, kg, vg)
     return (loss.reshape(()), hg.T, kg[None], vg[None])
 
 

time: 133 us -> 128 us (0.962)
  local copies, waits for them, and re-layouts: 4.37 us -> 0 us
    unnamed x7 -> x0, local copies, waits for them, and re-layouts: 4.37 us -> none
    pallas_call x1, Pallas kernels: 123 us -> 120 us  [body(): call(queries[0], enc_keys[0], enc_values[0], enc_lengths, out_proj, resid...]
    pallas_call x0 -> x1, Pallas kernels: none -> 2.52 us  [body(): pl.pallas_call(tail, out_shape=tuple((jax.ShapeDtypeStruct(x.shape, x.dty...]
where the time goes in v4:
time: 128 us; the launch traced here: 126 us
  Pallas kernels  123 us (96%)
  between operations  2.98 us (2%)
    pallas_call x1, Pallas kernels, body(): call(queries[0], enc_keys[0], enc_values[0], enc_lengths, out_proj, resid...  120 us

profile of v4, /device:TPU:1, one launch (start us, length us, event | category | flops | bytes accessed | tf_op | source)
XLA Modules:
  0.0 125.8 jit_solution(12438481201606388307)
XLA Ops:
  1.3 120.3 %shard_map.120 = (f32[1,1]{1,0:T(1,128)}, bf16[2008,512]{1,0:T(8,128)(2,1)}, f32[128,256]{1,0:T(8,128)}, f32[128,256]{1,0:T(8,128)}) custom-call(bf16[32,256]{1,0:T(8,128)(2,1)} %bitcast.14, bf16[128,256]{1,0:T(8,128)(2,1)} %bitcast.12, bf16[128,256]{1,0:T(8,128)(2,1)} %bitcast.13, s32[1]{0:T(128)S(6)} %copy.14.ln, bf16[256,512]{1,0:T(8,128)(2,1)} %wo_hbm.1, ...), custom_call_target="tpu_custom_call" | custom-call | tf_op jit(solution)/shard_map/pallas_call | solution.py:514
  121.6 2.5 %shard_map.121 = (bf16[2008,512]{1,0:T(8,128)(2,1)}, f32[128,256]{1,0:T(8,128)}, f32[128,256]{1,0:T(8,128)}) custom-call(bf16[2008,512]{1,0:T(8,128)(2,1)} %get-tuple-element.12.hg, f32[128,256]{1,0:T(8,128)} %get-tuple-element.13.kg, f32[128,256]{1,0:T(8,128)} %get-tuple-element.14.vg), custom_call_target="tpu_custom_call" | custom-call | tf_op jit(solution)/shard_map/pallas_call | solution.py:517

commit v5 on v4

--- a/solution.py
+++ b/solution.py
@@ -174,8 +174,6 @@
         att = att + b.acc_recv[i].astype(F32) * shares[i]
     b.att_all[ms] = att.astype(BF16)
     got_att = spread(b.att_all.at[ms], b.att_all, "seq")
-    got_stat = spread(b.stat_all.at[ms], b.stat_all, "seq")
-    got_full = scatter(b.full_send, b.full_recv, "seq")
     got_att()
 
     mixed_part = dot(b.att_all[...].reshape(R, HD), wo[...], 1, 0)
@@ -191,10 +189,8 @@
     got_mg = spread(b.mg.at[mv], b.mg, "vocab")
     b.sq[ms] = sub_pick([to_row(jnp.sum(mixed * mixed, axis=1, keepdims=True), RB)])
     got_sq = spread(b.sq.at[ms], b.sq, "seq")
-    got_sq()
-    square = jnp.sum(b.sq[...], axis=0)[0:1]
-    b.inv[mv] = sub_pick([lax.rsqrt(square / D + EPS)])
-    got_inv = spread(b.inv.at[mv], b.inv, "vocab")
+    got_stat = spread(b.stat_all.at[ms], b.stat_all, "seq")
+    got_full = scatter(b.full_send, b.full_recv, "seq")
     got_mg()
 
     def rows_of(owner):
@@ -213,6 +209,10 @@
         way = i // 2
         sends[way][0, i] = dot(far, w[part[i]], 1, 1)
         gots[way][0, i] = one(sends[way].at[0, i], recvs[way].at[0, i], "seq", toward[way])
+    got_sq()
+    square = jnp.sum(b.sq[...], axis=0)[0:1]
+    b.inv[mv] = sub_pick([lax.rsqrt(square / D + EPS)])
+    got_inv = spread(b.inv.at[mv], b.inv, "vocab")
     for step in range(1, H):
         both = jnp.concatenate([rows_of(at(H - step)), rows_of(at(step - H))], axis=0)
         for i in range(4):
@@ -239,7 +239,6 @@
     for i in range(NV):
         normed.append(b.mg[i].astype(F32) * to_col(b.inv[i][0:1], RB))
     b.normed[zlo] = jnp.concatenate(normed, axis=0).astype(BF16)
-    got_normed = one(b.normed.at[zlo], b.normed.at[zlo], "dp", zmate)
     inv_own = jnp.concatenate([to_col(b.inv[ms * NB + i][0:1], RB) for i in range(NB)], axis=0)
     for i in range(4):
         block = b.logits[:, part[i]]
@@ -282,7 +281,6 @@
     for i in range(4):
         g_all[ms, i] = grad[:, i * VQ:(i + 1) * VQ]
 
-    got_z = one(g_all.at[ms], g_all.at[ms], "dp", zmate)
 
     def ring(buf):
         cw_got, cc_got = {}, {}
@@ -330,17 +328,19 @@
         forward(step)
         if step == 0:
             got_along = spread(b.along.at[mv], b.along, "vocab")
+            got_z = one(g_all.at[ms], g_all.at[ms], "dp", zmate)
+            got_normed = one(b.normed.at[zlo], b.normed.at[zlo], "dp", zmate)
             hidden([ms])
         else:
             hidden([at(-step), at(step)])
-        if step == min(1, H - 1):
+        if step == min(2, H - 1):
             got_along()
             b.loss[ms] = sub_pick([loss, jnp.sum(b.along[...], axis=0)[0:1]])
             got_loss = spread(b.loss.at[ms], b.loss, "seq")
+    last()
+    hidden([at(H)])
     got_z()
     far_forward(0)
-    last()
-    hidden([at(H)])
     for step in range(1, min(2, H)):
         far_forward(step)
 

time: 128 us -> 126 us (0.984)
  the two profiles are of different devices: /device:TPU:1 before, /device:TPU:2 now
where the time goes in v5:
time: 126 us
  Pallas kernels  123 us (98%)
  between operations  2.98 us (2%)
    pallas_call x1, Pallas kernels, body(): call(queries[0], enc_keys[0], enc_values[0], enc_lengths, out_proj, resid...  121 us

profile of v5, /device:TPU:2, one launch (start us, length us, event | category | flops | bytes accessed | tf_op | source)
XLA Modules:
  0.0 126.3 jit_solution(11969493995990494193)
XLA Ops:
  1.3 120.8 %shard_map.120 = (f32[1,1]{1,0:T(1,128)}, bf16[2008,512]{1,0:T(8,128)(2,1)}, f32[128,256]{1,0:T(8,128)}, f32[128,256]{1,0:T(8,128)}) custom-call(bf16[32,256]{1,0:T(8,128)(2,1)} %bitcast.14, bf16[128,256]{1,0:T(8,128)(2,1)} %bitcast.12, bf16[128,256]{1,0:T(8,128)(2,1)} %bitcast.13, s32[1]{0:T(128)S(6)} %copy.14.ln, bf16[256,512]{1,0:T(8,128)(2,1)} %wo_hbm.1, ...), custom_call_target="tpu_custom_call" | custom-call | tf_op jit(solution)/shard_map/pallas_call | solution.py:514
  122.0 2.5 %shard_map.121 = (bf16[2008,512]{1,0:T(8,128)(2,1)}, f32[128,256]{1,0:T(8,128)}, f32[128,256]{1,0:T(8,128)}) custom-call(bf16[2008,512]{1,0:T(8,128)(2,1)} %get-tuple-element.12.hg, f32[128,256]{1,0:T(8,128)} %get-tuple-element.13.kg, f32[128,256]{1,0:T(8,128)} %get-tuple-element.14.vg), custom_call_target="tpu_custom_call" | custom-call | tf_op jit(solution)/shard_map/pallas_call | solution.py:517
